TPU v7x, 128 devices: a whole 4x4x4 slice. The times are simulated.
128 devices in a mesh: space: 16 (over z, y_hi, core), tm: 8 (over y_lo, x).
Axes of the slice: x: 4, y: 4 (y_hi: 2, y_lo: 2; y = y_hi * 2 + y_lo), z: 4, core: 2. Of those that a mesh axis runs over, the one named last changes fastest.
Arguments:
- gauge_links: float32 [4, 2, 3, 3, 32, 64, 256], P(None, None, None, None, 'tm', 'space'), may hold values from -1 to 1, as said below
Outputs:
- flowed_links: float32 [4, 2, 3, 3, 32, 64, 256], P(None, None, None, None, 'tm', 'space')
- flow_force: float32 [4, 2, 3, 3, 32, 64, 256], P(None, None, None, None, 'tm', 'space')
- holonomy: float32 [2, 3, 3, 8, 64, 256], P(None, None, None, 'tm', 'space')
Inputs may be any that keep to these rules, and one draw needn't show every extreme that they name: `gauge_links`: every link is a special unitary 3 x 3 matrix.
All inputs are finite; a program needn't handle non-finite values.
Results may differ from a plain program's by a relative error of at most 0.00002.
Values sent between devices are 32-bit elements; how exact they have to be, the bound alone decides.
No kernel may reach another device: no remote copies, remote signals or barrier semaphores. Data moves between devices by JAX's collectives and lax.ppermute only.
A program may use at most 64 MiB of HBM per device.

v0:
```python
import jax
import jax.numpy as jnp
from jax import lax
from jax.experimental import pallas as pl
from jax.experimental.pallas import tpu as pltpu
from jax.sharding import PartitionSpec as P


F32 = jnp.float32
VMEM = pltpu.VMEM
PAIRS = ((0, 1), (0, 2), (1, 2))
ROW = 4


def entry(terms):
    re = im = None
    for (ar, ai), ca, (br, bi), cb in terms:
        p = ar * br
        q = ai * bi
        re = p if re is None else re + p
        re = re + q if ca != cb else re - q
        u = ar * bi
        v = ai * br
        if im is None:
            im = (v - u) if cb and not ca else (u - v) if ca and not cb else (u + v)
        else:
            im = im - u if cb else im + u
            im = im - v if ca else im + v
    return re, im


def entry_im(terms):
    im = None
    for (ar, ai), ca, (br, bi), cb in terms:
        u = ar * bi
        v = ai * br
        if im is None:
            im = (v - u) if cb and not ca else (u - v) if ca and not cb else (u + v)
        else:
            im = im - u if cb else im + u
            im = im - v if ca else im + v
    return im


def terms(a, ha, b, hb, i, j):
    out = []
    for k in range(3):
        x = a[k][i] if ha else a[i][k]
        y = b[j][k] if hb else b[k][j]
        out.append((x, ha, y, hb))
    return out


def product(a, b, ha=False, hb=False):
    return [[entry(terms(a, ha, b, hb, i, j)) for j in range(3)] for i in range(3)]


def twice_ta(a, b):
    out = []
    for i, j in PAIRS:
        r1, i1 = entry(terms(a, False, b, False, i, j))
        r2, i2 = entry(terms(a, False, b, False, j, i))
        out += [r1 - r2, i1 + i2]
    d = [entry_im(terms(a, False, b, False, k, k)) for k in range(3)]
    tr = (d[0] + d[1] + d[2]) * (2.0 / 3.0)
    return out + [d[0] + d[0] - tr, d[1] + d[1] - tr]


def transport(u, c):
    r01, i01, r02, i02, r12, i12, d0, d1 = c
    d2 = -(d0 + d1)
    off = {(0, 1): (r01, i01), (0, 2): (r02, i02), (1, 2): (r12, i12)}
    diag = (d0, d1, d2)
    t = []
    for i in range(3):
        row = []
        for j in range(3):
            ur, ui = u[i][j]
            re = -(ui * diag[j])
            im = ur * diag[j]
            for k in range(3):
                if k == j:
                    continue
                ar, ai = u[i][k]
                if k < j:
                    cr, ci = off[k, j]
                    re = re + ar * cr - ai * ci
                    im = im + ar * ci + ai * cr
                else:
                    cr, ci = off[j, k]
                    re = re - ar * cr - ai * ci
                    im = im + ar * ci - ai * cr
            row.append((re, im))
        t.append(row)
    out = []
    for i, j in PAIRS:
        out += list(entry(terms(t, False, u, True, i, j)))
    for k in range(2):
        out.append(entry_im(terms(t, False, u, True, k, k)))
    return out


def taylor(f):
    r01, i01, r02, i02, r12, i12, h0, h1 = f
    h2 = -(h0 + h1)
    n01 = r01 * r01 + i01 * i01
    n02 = r02 * r02 + i02 * i02
    n12 = r12 * r12 + i12 * i12
    y0 = -(h0 * h0 + n01 + n02)
    y1 = -(h1 * h1 + n01 + n12)
    y2 = -(h2 * h2 + n02 + n12)
    s = 0.5 * (y0 + y1 + y2)
    y01 = (h2 * i01 - (r02 * r12 + i02 * i12), -(h2 * r01) - (i02 * r12 - r02 * i12))
    y02 = (h1 * i02 + (r01 * r12 - i01 * i12), -(h1 * r02) + (r01 * i12 + i01 * r12))
    y12 = (h0 * i12 - (r01 * r02 + i01 * i02), -(h0 * r12) - (r01 * i02 - i01 * r02))
    zr = r01 * r12 - i01 * i12
    zi = r01 * i12 + i01 * r12
    trip = zi * r02 - zr * i02
    e = -(h0 * h1 * h2 + (trip + trip) - h0 * n12 - h1 * n02 - h2 * n01)
    q0r = 1.0 - e * e * (1.0 / 720.0)
    q0i = e * (1.0 / 6.0 + s * (1.0 / 120.0))
    q1r = 1.0 + s * (1.0 / 6.0 + s * (1.0 / 120.0))
    q1i = e * (1.0 / 24.0 + s * (1.0 / 360.0))
    q2r = 0.5 + s * (1.0 / 24.0 + s * (1.0 / 720.0))
    q2i = e * (1.0 / 120.0)
    out = [[None] * 3 for _ in range(3)]
    offs = (((r01, i01), y01), ((r02, i02), y02), ((r12, i12), y12))
    for (i, j), ((xr, xi), (yr, yi)) in zip(PAIRS, offs):
        p1, p2, p3, p4 = q1r * xr, q1i * xi, q1r * xi, q1i * xr
        s1, s2, s3, s4 = q2r * yr, q2i * yi, q2r * yi, q2i * yr
        out[i][j] = ((p1 - p2) + (s1 - s2), (p3 + p4) + (s3 + s4))
        out[j][i] = ((s1 + s2) - (p1 + p2), (p3 - p4) + (s4 - s3))
    for k, (h, y) in enumerate(((h0, y0), (h1, y1), (h2, y2))):
        out[k][k] = (q0r - q1i * h + q2r * y, q0i + q1r * h + q2i * y)
    return out


def masks():
    lane = lax.broadcasted_iota(jnp.int32, (8, 128), 1)
    z = lax.broadcasted_iota(jnp.int32, (8, 128), 0) & 3
    return {"x": lane & 15, "y": lane >> 4, "z": z}


def shift_x(v, m, up):
    if up:
        return jnp.where(m["x"] == 15, pltpu.roll(v, 15, 1), pltpu.roll(v, 127, 1))
    return jnp.where(m["x"] == 0, pltpu.roll(v, 113, 1), pltpu.roll(v, 1, 1))


def shift_y(v, m, up):
    r = pltpu.roll(v, 112 if up else 16, 1)
    return jnp.where(m["y"] == (7 if up else 0), pltpu.roll(r, 4, 0), r)


def mat(fetch):
    return [[(fetch(0, i, j), fetch(1, i, j)) for j in range(3)] for i in range(3)]


def on_mat(m, f):
    return [[(f(a), f(b)) for a, b in row] for row in m]


def plane(u_mu, u_nu, mu_up, nu_up):
    d = product(u_mu, u_nu, ha=True)
    g = product(mu_up, nu_up, hb=True)
    return twice_ta(g, d), twice_ta(d, g)


def unpack_rows(ref, base):
    m = [[(ref[base * 12 + i * 3 + j], ref[base * 12 + 6 + i * 3 + j]) for j in range(3)] for i in range(2)]
    third = []
    for k in range(3):
        a, b = (k + 1) % 3, (k + 2) % 3
        r1, i1 = entry([(m[0][a], False, m[1][b], False)])
        r2, i2 = entry([(m[0][b], False, m[1][a], False)])
        third.append((r1 - r2, i2 - i1))
    return m + [third]


def tiles(ref, shape):
    return ref.reshape(*shape, 8, 128)


def load_kernel(u_hbm, u_ref, st_ref, szt_ref, szxy_ref, sem):
    copies = {}
    for d in (3, 0, 1, 2):
        for h in range(2):
            src = u_hbm.at[d, :, :, :, :, :, pl.ds(128 * h, 128)]
            copies[d, h] = pltpu.make_async_copy(src, u_ref.at[d, :, :, :, :, h], sem.at[d, h])
            copies[d, h].start()
    u = tiles(u_ref, (4, 2, 3, 3, 4))
    rows = u_ref.reshape(4, 2, 3, 3, 32, 128)
    for d in (3, 0, 1, 2):
        for h in range(2):
            copies[d, h].wait()
        for p in range(2):
            for i in range(2):
                for j in range(3):
                    k = p * 6 + i * 3 + j
                    if d < 3:
                        st_ref[d * 12 + k] = u[d, p, i, j, 0]
                    if d < 2:
                        szxy_ref[d * 12 + k] = rows[d, p, i, j, pl.ds(0, 8, stride=4), :]
                    if d == 3:
                        szt_ref[k] = rows[d, p, i, j, pl.ds(0, 8, stride=4), :]


def accumulate(ref, mu, t, vals, sign=1):
    for k in range(8):
        if sign > 0:
            ref[mu, k, t] += vals[k]
        else:
            ref[mu, k, t] -= vals[k]


def inside(vals, m):
    return [jnp.where(m["z"] == 3, 0.0, v) for v in vals]


def next_z(v):
    return pltpu.roll(v, 7, 0)


def down_z(v, m):
    return jnp.where(m["z"] == 0, 0.0, pltpu.roll(v, 1, 0))


def links(u):
    return lambda d, t: mat(lambda p, i, j: u[d, p, i, j, t])


def side_z(c_ref, r_ref, mu, shift, m, t, u_mu, u_z):
    a, b = plane(u_mu, u_z, on_mat(u_mu, next_z), on_mat(u_z, lambda v: shift(v, m, True)))
    b = inside(b, m)
    accumulate(c_ref, 2, t, inside(a, m))
    accumulate(c_ref, mu, t, b, -1)
    accumulate(r_ref, mu, t, [down_z(v, m) for v in a])
    accumulate(r_ref, 2, t, [shift(v, m, False) for v in b], -1)


def zt_inside(c_ref, r_ref, m, t, u_z, u_t, z_up):
    a, b = plane(u_z, u_t, z_up, on_mat(u_t, next_z))
    a = inside(a, m)
    accumulate(c_ref, 3, t, a)
    accumulate(c_ref, 2, t, inside(b, m), -1)
    accumulate(r_ref, 2, t + 1, a)
    accumulate(r_ref, 3, t, [down_z(v, m) for v in b], -1)


def inner_kernel(u_ref, c_ref, r_ref):
    link = links(tiles(u_ref, (4, 2, 3, 3, 4)))
    m = masks()
    c_ref[...] = jnp.zeros_like(c_ref)
    r_ref[...] = jnp.zeros_like(r_ref)

    def spatial(t, carry):
        ux, uy, uz = link(0, t), link(1, t), link(2, t)
        a, b = plane(ux, uy, on_mat(ux, lambda v: shift_y(v, m, True)), on_mat(uy, lambda v: shift_x(v, m, True)))
        accumulate(c_ref, 1, t, a)
        accumulate(c_ref, 0, t, b, -1)
        accumulate(r_ref, 0, t, [shift_y(v, m, False) for v in a])
        accumulate(r_ref, 1, t, [shift_x(v, m, False) for v in b], -1)
        side_z(c_ref, r_ref, 0, shift_x, m, t, ux, uz)
        side_z(c_ref, r_ref, 1, shift_y, m, t, uy, uz)
        return carry

    lax.fori_loop(0, 4, spatial, 0)

    def timelike(t, carry):
        for mu, shift in ((0, shift_x), (1, shift_y)):
            side_time(c_ref, r_ref, mu, shift, m, t, link(mu, t), link(3, t), link(mu, t + 1))
        zt_inside(c_ref, r_ref, m, t, link(2, t), link(3, t), link(2, t + 1))
        return carry

    lax.fori_loop(0, 3, timelike, 0)


def side_time(c_ref, r_ref, mu, shift, m, t, u_mu, u_t, mu_up):
    a, b = plane(u_mu, u_t, mu_up, on_mat(u_t, lambda v: shift(v, m, True)))
    accumulate(c_ref, 3, t, a)
    accumulate(c_ref, mu, t, b, -1)
    accumulate(r_ref, mu, t + 1, a)
    accumulate(r_ref, 3, t, [shift(v, m, False) for v in b], -1)


LAST = pl.ds(3, 8, stride=4)


def edge_kernel(u_ref, ht_ref, hzt_ref, after_ref, fzt_ref, ab_ref, uz4_ref, pk_ref):
    rows = u_ref.reshape(4, 2, 3, 3, 32, 128)
    above = unpack_rows(ht_ref, 2)
    for p in range(2):
        for i in range(3):
            for j in range(3):
                uz4_ref[p, i, j] = above[i][j][p]
                pk_ref[p, i, j, pl.ds(0, 6), :] = rows[2, p, i, j, pl.ds(11, 6, stride=4), :]
                pk_ref[p, i, j, pl.ds(6, 2), :] = uz4_ref[p, i, j, pl.ds(3, 2, stride=4), :]
    uz = mat(lambda p, i, j: rows[2, p, i, j, LAST, :])
    ut = mat(lambda p, i, j: rows[3, p, i, j, LAST, :])
    a, b = plane(uz, ut, mat(lambda p, i, j: pk_ref[p, i, j]), unpack_rows(hzt_ref, 0))
    for k in range(8):
        fzt_ref[k] = -b[k]
        ab_ref[k] = a[k]
        ab_ref[8 + k] = b[k]


def expand(x_ref, n, tile, offset):
    x_ref[n] = jnp.zeros((32, 128), F32)
    x_ref[n, pl.ds(offset, 8, stride=4), :] = tile


def at(t):
    return pl.ds(t * 8 if isinstance(t, int) else pl.multiple_of(t * 8, 8), 8)


def middle_kernel(u_ref, ht_ref, uz4_ref, ab_ref, c_in, r_in, c_ref, r_ref, f_ref, ft_ref, x_ref):
    link = links(tiles(u_ref, (4, 2, 3, 3, 4)))
    m = masks()
    for k in range(16):
        expand(x_ref, k, ab_ref[k], 3)
    for k in range(8):
        for t in range(4):
            a = x_ref[k, at(t), :]
            c_ref[3, k, t] += a
            c_ref[2, k, t] -= x_ref[8 + k, at(t), :]
            r_ref[2, k, t + 1] += a
    for mu, shift in ((0, shift_x), (1, shift_y)):
        side_time(c_ref, r_ref, mu, shift, m, 3, link(mu, 3), link(3, 3), unpack_rows(ht_ref, mu))
    zt_inside(c_ref, r_ref, m, 3, link(2, 3), link(3, 3), get18(uz4_ref))
    for mu in range(3):
        for k in range(8):
            ft_ref[mu * 8 + k] = r_ref[mu, k, 4]

    def body(t, carry):
        w = transport(link(3, t), [c_ref[3, k, t] for k in range(8)])
        for k in range(8):
            f_ref[k, t] = w[k] + r_ref[3, k, t]
        return carry

    lax.fori_loop(0, 4, body, 0)


def packed_shift_y(v, m, up):
    r = pltpu.roll(v, 112 if up else 16, 1)
    other = jnp.where(m["odd"], pltpu.roll(r, 1, 0), pltpu.roll(r, 7, 0))
    return jnp.where(m["y"] == (7 if up else 0), other, r)


def late_edge_kernel(u_ref, hzxy_ref, after_ref, fz_ref, p_ref):
    rows = u_ref.reshape(4, 2, 3, 3, 32, 128)
    m = masks()
    m["odd"] = (lax.broadcasted_iota(jnp.int32, (8, 128), 0) & 1) == 1
    uz = mat(lambda p, i, j: rows[2, p, i, j, LAST, :])
    for mu, shift in ((0, shift_x), (1, packed_shift_y)):
        um = mat(lambda p, i, j: rows[mu, p, i, j, LAST, :])
        a, b = plane(um, uz, unpack_rows(hzxy_ref, mu), on_mat(uz, lambda v: shift(v, m, True)))
        for k in range(8):
            fz_ref[mu * 8 + k] = a[k]
            p_ref[mu * 8 + k] = b[k]
            back = shift(b[k], m, False)
            p_ref[16 + k] = a[k] if mu == 0 else p_ref[16 + k] + a[k]
            p_ref[24 + k] = back if mu == 0 else p_ref[24 + k] + back


def space_sum_kernel(u_ref, c_ref, r_ref, p_ref, after_ref, f_ref, x_ref):
    link = links(tiles(u_ref, (4, 2, 3, 3, 4)))
    for k in range(32):
        expand(x_ref, k, p_ref[k], 3)

    def body(t, carry):
        for mu in range(3):
            x = [x_ref[(16 if mu == 2 else mu * 8) + k, at(t), :] for k in range(8)]
            c = [c_ref[mu, k, t] for k in range(8)]
            w = transport(link(mu, t), [a + b if mu == 2 else a - b for a, b in zip(c, x)])
            for k in range(8):
                v = w[k] + r_ref[mu, k, t]
                f_ref[mu, k, t] = v - x_ref[24 + k, at(t), :] if mu == 2 else v
        return carry

    lax.fori_loop(0, 4, body, 0)


def finish(f, u, z_out, new_out):
    z = [-0.5 * v for v in f]
    zero = jnp.zeros_like(z[0])
    for n, (i, j) in enumerate(PAIRS):
        z_out(0, i, j, z[2 * n])
        z_out(1, i, j, z[2 * n + 1])
        z_out(0, j, i, -z[2 * n])
        z_out(1, j, i, z[2 * n + 1])
    for k, d in enumerate((z[6], z[7], -(z[6] + z[7]))):
        z_out(0, k, k, zero)
        z_out(1, k, k, d)
    new = product(taylor([0.125 * v for v in z]), u)
    for i in range(3):
        for j in range(3):
            for p in range(2):
                new_out(p, i, j, new[i][j][p])
    return new


def writer(ref, *head, t):
    def put(p, i, j, v):
        ref[(*head, p, i, j, t)] = v

    return put


def time_kernel(u_ref, f_ref, fz_ref, after_ref, zt_ref, nt_ref, s_ref, x_ref):
    link = links(tiles(u_ref, (4, 2, 3, 3, 4)))
    zt, nt = tiles(zt_ref, (2, 3, 3, 4)), tiles(nt_ref, (2, 3, 3, 4))
    for k in range(8):
        expand(x_ref, k, fz_ref[k], 0)

    def body(t, carry):
        f = [f_ref[k, t] + x_ref[k, at(t), :] for k in range(8)]
        finish(f, link(3, t), writer(zt, t=t), writer(nt, t=t))
        return carry

    lax.fori_loop(0, 4, body, 0)
    slab = mat(lambda p, i, j: nt[p, i, j, 0])
    for t in range(1, 4):
        slab = product(slab, mat(lambda p, i, j: nt[p, i, j, t]))
    put18(s_ref, slab)


def out_copies(src, dst, sem, d):
    return [pltpu.make_async_copy(src.at[:, :, :, :, h], dst.at[d, :, :, :, :, :, pl.ds(128 * h, 128)], sem.at[h]) for h in range(2)]


def space_kernel(u_ref, f_ref, fz_ref, ft_ref, zt_ref, nt_ref, new_hbm, z_hbm, zs_ref, ns_ref, x_ref, sem):
    link = links(tiles(u_ref, (4, 2, 3, 3, 4)))
    copies = out_copies(zt_ref, z_hbm, sem.at[6], 3) + out_copies(nt_ref, new_hbm, sem.at[7], 3)
    for c in copies:
        c.start()
    for k in range(16):
        expand(x_ref, k, fz_ref[k], 0)
    for k in range(24):
        f_ref[k // 8, k % 8, 0] += ft_ref[k]
    for mu in range(3):
        zs, ns = tiles(zs_ref.at[mu], (2, 3, 3, 4)), tiles(ns_ref.at[mu], (2, 3, 3, 4))

        def body(t, carry):
            f = [f_ref[mu, k, t] for k in range(8)]
            if mu < 2:
                f = [v + x_ref[mu * 8 + k, at(t), :] for k, v in enumerate(f)]
            finish(f, link(mu, t), writer(zs, t=t), writer(ns, t=t))
            return carry

        lax.fori_loop(0, 4, body, 0)
        more = out_copies(zs_ref.at[mu], z_hbm, sem.at[2 * mu], mu) + out_copies(ns_ref.at[mu], new_hbm, sem.at[2 * mu + 1], mu)
        for c in more:
            c.start()
        copies += more
    for c in copies:
        c.wait()


def get18(ref):
    return mat(lambda p, i, j: ref[p, i, j])


def put18(ref, m):
    for i in range(3):
        for j in range(3):
            for p in range(2):
                ref[p, i, j] = m[i][j][p]


def chain(mats):
    out = mats[0]
    for x in mats[1:]:
        out = product(out, x)
    return out


def join_kernel(s0_ref, s1_ref, s2_ref, s3_ref, head_ref, tail_ref, row_ref):
    x = lax.rem(lax.axis_index("tm"), ROW)
    cyc = [s0_ref, s1_ref, s2_ref, s3_ref]
    for n in range(ROW):

        @pl.when(x == n)
        def _():
            head = chain([get18(r) for r in cyc[: ROW - n]])
            put18(head_ref, head)
            if n == 0:
                put18(row_ref, head)
                one, zero = jnp.ones((8, 128), F32), jnp.zeros((8, 128), F32)
                put18(tail_ref, [[(one if i == j else zero, zero) for j in range(3)] for i in range(3)])
            else:
                tail = chain([get18(r) for r in cyc[ROW - n :]])
                put18(tail_ref, tail)
                put18(row_ref, product(tail, head))


def holonomy_kernel(head_ref, row_ref, tail_ref, out_hbm, o_ref, sem):
    loop = product(product(get18(head_ref), get18(row_ref)), get18(tail_ref))
    put18(tiles(o_ref, (2, 3, 3)), loop)
    copies = []
    for h in range(2):
        copies.append(pltpu.make_async_copy(o_ref.at[:, :, :, h], out_hbm.at[:, :, :, 0, :, pl.ds(128 * h, 128)], sem.at[h]))
    for c in copies:
        c.start()
    for c in copies:
        c.wait()


def call(kernel, outs, args, scratch=(), aliases=None, us=1.0):
    def spec(kind):
        return pl.BlockSpec(memory_space=VMEM if kind == "v" else pltpu.HBM)

    shapes = [VMEM(s, F32) if kind == "v" else jax.ShapeDtypeStruct(s, F32) for kind, s in outs]
    values = [pltpu.with_memory_space_constraint(x, VMEM if kind == "v" else pltpu.HBM) for kind, x in args]
    return pl.pallas_call(
        kernel,
        out_shape=shapes,
        in_specs=[spec(k) for k, _ in args],
        out_specs=[spec(k) for k, _ in outs],
        scratch_shapes=list(scratch),
        input_output_aliases=aliases or {},
        compiler_params=pltpu.CompilerParams(vmem_limit_bytes=24 << 20),
        cost_estimate=pl.CostEstimate(flops=int(us * 1e6), bytes_accessed=int(us * 3e6), transcendentals=0),
    )(*values)


def from_ahead(x, axis, k):
    n = lax.axis_size(axis)
    return lax.ppermute(x, axis, [(i, (i - k) % n) for i in range(n)])


def in_row(x, k):
    n = lax.axis_size("tm")
    return lax.ppermute(x, "tm", [(i, i // ROW * ROW + (i - k) % ROW) for i in range(n)])


def program(gauge_links):
    dma = pltpu.SemaphoreType.DMA
    whole = (4, 2, 3, 3, 4, 2, 4, 128)
    mat18 = ("v", (2, 3, 3, 8, 128))
    full = ("h", gauge_links.shape)

    def packed(n):
        return ("v", (n, 8, 128))

    u, st, szt, szxy = call(load_kernel, [("v", whole), packed(36), packed(12), packed(24)], [("h", gauge_links)], [dma((4, 2))])
    u = ("v", u)
    hzt = ("v", from_ahead(szt, "space", 1))
    ht = ("v", from_ahead(st, "tm", 1))
    hzxy = ("v", from_ahead(szxy, "space", 1))
    acc = [("v", (4, 8, 4, 8, 128)), ("v", (4, 8, 5, 8, 128))]
    c, r = call(inner_kernel, acc, [u], us=4.0)
    fzt, ab, uz4 = call(edge_kernel, [packed(8), packed(16), mat18], [u, ht, hzt, ("v", c)], [VMEM((2, 3, 3, 8, 128), F32)], us=0.3)
    fzt = ("v", from_ahead(fzt, "space", -1))
    c, r, f3, ft = call(
        middle_kernel,
        [*acc, ("v", (8, 4, 8, 128)), packed(24)],
        [u, ht, ("v", uz4), ("v", ab), ("v", c), ("v", r)],
        [VMEM((16, 32, 128), F32)],
        {4: 0, 5: 1},
    )
    ft = ("v", from_ahead(ft, "tm", -1))
    fz, p = call(late_edge_kernel, [packed(16), packed(32)], [u, hzxy, ("v", f3)], us=0.5)
    fz = ("v", from_ahead(fz, "space", -1))
    slices = ("v", (2, 3, 3, 4, 2, 4, 128))
    zt, nt, s = call(time_kernel, [slices, slices, mat18], [u, ("v", f3), fzt, ("v", p)], [VMEM((8, 32, 128), F32)], us=0.4)
    s1, s3, s2 = in_row(s, 1), in_row(s, 3), in_row(s, 2)
    (f,) = call(space_sum_kernel, [("v", (3, 8, 4, 8, 128))], [u, ("v", c), ("v", r), ("v", p), ("v", s)], [VMEM((32, 32, 128), F32)], us=1.0)
    head, tail, row = call(join_kernel, [mat18] * 3, [("v", s), ("v", s1), ("v", s2), ("v", s3)], us=0.1)
    row = from_ahead(row, "tm", ROW)
    stage = VMEM((3, 2, 3, 3, 4, 2, 4, 128), F32)
    new, force = call(
        space_kernel,
        [full, full],
        [u, ("v", f), fz, ft, ("v", zt), ("v", nt)],
        [stage, stage, VMEM((16, 32, 128), F32), dma((8, 2))],
        us=3.0,
    )
    (hol,) = call(
        holonomy_kernel,
        [("h", (2, 3, 3, 1, *gauge_links.shape[5:]))],
        [("v", head), ("v", row), ("v", tail)],
        [VMEM((2, 3, 3, 2, 4, 128), F32), dma((2,))],
    )
    return new, force, hol


def solution(mesh):
    in_specs = (P(None, None, None, None, "tm", "space", None),)
    out_specs = (
        P(None, None, None, None, "tm", "space", None),
        P(None, None, None, None, "tm", "space", None),
        P(None, None, None, "tm", "space", None),
    )
    return jax.shard_map(program, mesh=mesh, in_specs=in_specs, out_specs=out_specs, check_vma=False)
```

profile of v0, /device:TPU:0, one launch (start us, length us, event | category | flops | bytes accessed | tf_op | source)
XLA Modules:
  0.0 40.6 jit_solution(2060065310409500213)
XLA Ops:
  0.6 1.4 %shard_map.38 = (f32[4,2,3,3,4,2,4,128]{7,6,5,4,3,2,1,0:T(4,128)S(1)}, f32[36,8,128]{2,1,0:T(8,128)S(1)}, f32[12,8,128]{2,1,0:T(8,128)S(1)}, f32[24,8,128]{2,1,0:T(8,128)S(1)}) custom-call(f32[4,2,3,3,4,4,256]{6,5,4,3,2,1,0:T(4,128)} %u_hbm.1), custom_call_target="tpu_custom_call" | custom-call | flops 1000000 | bytes 3000000 | tf_op jit(solution)/shard_map/pallas_call | solution.py:514
  2.0 4.0 %collective-permute-start = (f32[36,8,128]{2,1,0:T(8,128)S(1)}, f32[36,8,128]{2,1,0:T(8,128)S(1)}, u32[]{:S(2)}, u32[]{:S(2)}) collective-permute-start(f32[36,8,128]{2,1,0:T(8,128)S(1)} %get-tuple-element.27), channel_id=1, source_target_pairs={{0,7},{1,0},{2,1},{3,2},{4,3},{5,4},{6,5},{7,6},{8,15},{9,8},{10,9... | collective-permute-start | bytes 442376 | tf_op jit(solution)/shard_map/ppermute | solution.py:528
  6.0 5.5 %collective-permute-start.2 = (f32[24,8,128]{2,1,0:T(8,128)S(1)}, f32[24,8,128]{2,1,0:T(8,128)S(1)}, u32[]{:S(2)}, u32[]{:S(2)}) collective-permute-start(f32[24,8,128]{2,1,0:T(8,128)S(1)} %get-tuple-element.35), channel_id=1, source_target_pairs={{0,120},{8,0},{16,8},{24,16},{32,24},{40,32},{48,40},{56,48},{64,5... | collective-permute-start | bytes 294920 | tf_op jit(solution)/shard_map/ppermute | solution.py:528
  11.5 1.0 %collective-permute-start.1 = (f32[12,8,128]{2,1,0:T(8,128)S(1)}, f32[12,8,128]{2,1,0:T(8,128)S(1)}, u32[]{:S(2)}, u32[]{:S(2)}) collective-permute-start(f32[12,8,128]{2,1,0:T(8,128)S(1)} %get-tuple-element.28), channel_id=1, source_target_pairs={{0,120},{8,0},{16,8},{24,16},{32,24},{40,32},{48,40},{56,48},{64,5... | collective-permute-start | bytes 147464 | tf_op jit(solution)/shard_map/ppermute | solution.py:528
  12.5 3.2 %shard_map.39 = (f32[4,8,4,8,128]{4,3,2,1,0:T(8,128)S(1)}, f32[4,8,5,8,128]{4,3,2,1,0:T(8,128)S(1)}) custom-call(f32[4,2,3,3,4,2,4,128]{7,6,5,4,3,2,1,0:T(4,128)S(1)} %get-tuple-element.26.u_ref), custom_call_target="tpu_custom_call" | custom-call | flops 4000000 | bytes 12000000 | tf_op jit(solution)/shard_map/pallas_call | solution.py:514
  15.7 0.0 collective-permute-done.1.hzt_ref
  15.7 0.0 collective-permute-done.ht_ref
  15.7 0.1 shard_map.40
  15.8 0.1 collective-permute-start.3
  15.9 0.6 %shard_map.41 = (f32[4,8,4,8,128]{4,3,2,1,0:T(8,128)S(1)}, f32[4,8,5,8,128]{4,3,2,1,0:T(8,128)S(1)}, f32[8,4,8,128]{3,2,1,0:T(8,128)S(1)}, f32[24,8,128]{2,1,0:T(8,128)S(1)}) custom-call(f32[4,2,3,3,4,2,4,128]{7,6,5,4,3,2,1,0:T(4,128)S(1)} %get-tuple-element.26.u_ref, ...), custom_call_target="tpu_custom_call", output_to_operand_aliasing={{0}: (4, {}), {1}: (5, {})} | custom-call | flops 1000000 | bytes 3000000 | tf_op jit(solution)/shard_map/pallas_call | solution.py:514
  16.5 0.0 collective-permute-done.2.hzxy_ref
  16.5 0.4 shard_map.42
  16.8 6.0 %collective-permute-done.3.fz_ref = f32[8,8,128]{2,1,0:T(8,128)S(1)} collective-permute-done((f32[8,8,128]{2,1,0:T(8,128)S(1)}, f32[8,8,128]{2,1,0:T(8,128)S(1)}, u32[]{:S(2)}, u32[]{:S(2)}) %collective-permute-start.3) | collective-permute-done | bytes 32800 | tf_op jit(solution)/shard_map/ppermute | solution.py:528
  22.8 0.4 shard_map.43
  23.2 0.1 collective-permute-start.8
  23.3 1.6 %collective-permute-start.7 = (f32[2,3,3,8,128]{4,3,2,1,0:T(8,128)S(1)}, f32[2,3,3,8,128]{4,3,2,1,0:T(8,128)S(1)}, u32[]{:S(2)}, u32[]{:S(2)}) collective-permute-start(f32[2,3,3,8,128]{4,3,2,1,0:T(8,128)S(1)} %get-tuple-element.39.after_ref.s0_ref), channel_id=1, source_target_pairs={{0,2},{1,3},{2,0},{3,1},{4,6},{5,7},{6,4},{7,5},{8,10},{9,11},{10,... | collective-permute-start | bytes 221192 | tf_op jit(solution)/shard_map/ppermute | solution.py:533
  24.9 1.7 %collective-permute-start.6 = (f32[2,3,3,8,128]{4,3,2,1,0:T(8,128)S(1)}, f32[2,3,3,8,128]{4,3,2,1,0:T(8,128)S(1)}, u32[]{:S(2)}, u32[]{:S(2)}) collective-permute-start(f32[2,3,3,8,128]{4,3,2,1,0:T(8,128)S(1)} %get-tuple-element.39.after_ref.s0_ref), channel_id=1, source_target_pairs={{0,3},{1,0},{2,1},{3,2},{4,7},{5,4},{6,5},{7,6},{8,11},{9,8},{10,9... | collective-permute-start | bytes 221192 | tf_op jit(solution)/shard_map/ppermute | solution.py:533
  26.5 0.9 %collective-permute-start.5 = (f32[24,8,128]{2,1,0:T(8,128)S(1)}, f32[24,8,128]{2,1,0:T(8,128)S(1)}, u32[]{:S(2)}, u32[]{:S(2)}) collective-permute-start(f32[24,8,128]{2,1,0:T(8,128)S(1)} %get-tuple-element.41), channel_id=1, source_target_pairs={{0,1},{1,2},{2,3},{3,4},{4,5},{5,6},{6,7},{7,0},{8,9},{9,10},{10,1... | collective-permute-start | bytes 294920 | tf_op jit(solution)/shard_map/ppermute | solution.py:528
  27.4 2.3 %collective-permute-done.8.s3_ref = f32[2,3,3,8,128]{4,3,2,1,0:T(8,128)S(1)} collective-permute-done((f32[2,3,3,8,128]{4,3,2,1,0:T(8,128)S(1)}, f32[2,3,3,8,128]{4,3,2,1,0:T(8,128)S(1)}, u32[]{:S(2)}, u32[]{:S(2)}) %collective-permute-start.8) | collective-permute-done | bytes 73760 | tf_op jit(solution)/shard_map/ppermute | solution.py:533
  29.6 0.0 collective-permute-done.7.s2_ref
  29.6 0.9 %collective-permute-done.6.s1_ref = f32[2,3,3,8,128]{4,3,2,1,0:T(8,128)S(1)} collective-permute-done((f32[2,3,3,8,128]{4,3,2,1,0:T(8,128)S(1)}, f32[2,3,3,8,128]{4,3,2,1,0:T(8,128)S(1)}, u32[]{:S(2)}, u32[]{:S(2)}) %collective-permute-start.6) | collective-permute-done | bytes 73760 | tf_op jit(solution)/shard_map/ppermute | solution.py:533
  30.5 0.1 shard_map.46
  30.6 0.2 collective-permute-start.9
  30.8 0.0 collective-permute-start.4
  30.8 0.5 %shard_map.44.f_ref = f32[3,8,4,8,128]{4,3,2,1,0:T(8,128)S(1)} custom-call(f32[4,2,3,3,4,2,4,128]{7,6,5,4,3,2,1,0:T(4,128)S(1)} %get-tuple-element.26.u_ref, f32[4,8,4,8,128]{4,3,2,1,0:T(8,128)S(1)} %get-tuple-element.33.c_ref, f32[4,8,5,8,128]{4,3,2,1,0:T(8,128)S(1)} %get-tuple-element.34.r_ref, f32[32,8,128]{2,1,0:T(8,128)S(1)} %get-tuple-element.37.after_ref.p_ref, ...), custom_call_target="tpu_custom_call" | custom-call | flops 1000000 | bytes 3000000 | tf_op jit(solution)/shard_map/pallas_call | solution.py:514
  31.3 6.8 %collective-permute-done.4.fz_ref = f32[16,8,128]{2,1,0:T(8,128)S(1)} collective-permute-done((f32[16,8,128]{2,1,0:T(8,128)S(1)}, f32[16,8,128]{2,1,0:T(8,128)S(1)}, u32[]{:S(2)}, u32[]{:S(2)}) %collective-permute-start.4) | collective-permute-done | bytes 65568 | tf_op jit(solution)/shard_map/ppermute | solution.py:528
  38.1 0.0 collective-permute-done.5.ft_ref
  38.1 1.7 %shard_map.45 = (f32[4,2,3,3,4,4,256]{6,5,4,3,2,1,0:T(4,128)}, f32[4,2,3,3,4,4,256]{6,5,4,3,2,1,0:T(4,128)}) custom-call(f32[4,2,3,3,4,2,4,128]{7,6,5,4,3,2,1,0:T(4,128)S(1)} %get-tuple-element.26.u_ref, f32[3,8,4,8,128]{4,3,2,1,0:T(8,128)S(1)} %shard_map.44.f_ref, f32[16,8,128]{2,1,0:T(8,128)S(1)} %collective-permute-done.4.fz_ref, ...), custom_call_target="tpu_custom_call" | custom-call | flops 3000000 | bytes 9000000 | tf_op jit(solution)/shard_map/pallas_call | solution.py:514
  39.9 0.0 collective-permute-done.9.row_ref
  39.9 0.7 %shard_map.47 = f32[2,3,3,1,4,256]{5,4,3,2,1,0:T(4,128)} custom-call(f32[2,3,3,8,128]{4,3,2,1,0:T(8,128)S(1)} %get-tuple-element.46.head_ref, f32[2,3,3,8,128]{4,3,2,1,0:T(8,128)S(1)} %collective-permute-done.9.row_ref, f32[2,3,3,8,128]{4,3,2,1,0:T(8,128)S(1)} %get-tuple-element.48.tail_ref), custom_call_target="tpu_custom_call" | custom-call | flops 1000000 | bytes 3000000 | tf_op jit(solution)/shard_map/pallas_call | solution.py:514
Async XLA Ops:
  2.0 13.6 %collective-permute-start = (f32[36,8,128]{2,1,0:T(8,128)S(1)}, f32[36,8,128]{2,1,0:T(8,128)S(1)}, u32[]{:S(2)}, u32[]{:S(2)}) collective-permute-start(f32[36,8,128]{2,1,0:T(8,128)S(1)} %get-tuple-element.27), channel_id=1, source_target_pairs={{0,7},{1,0},{2,1},{3,2},{4,3},{5,4},{6,5},{7,6},{8,15},{9,8},{10,9... | collective-permute-start | bytes 442376 | tf_op jit(solution)/shard_map/ppermute | solution.py:528
  6.0 10.5 %collective-permute-start.2 = (f32[24,8,128]{2,1,0:T(8,128)S(1)}, f32[24,8,128]{2,1,0:T(8,128)S(1)}, u32[]{:S(2)}, u32[]{:S(2)}) collective-permute-start(f32[24,8,128]{2,1,0:T(8,128)S(1)} %get-tuple-element.35), channel_id=1, source_target_pairs={{0,120},{8,0},{16,8},{24,16},{32,24},{40,32},{48,40},{56,48},{64,5... | collective-permute-start | bytes 294920 | tf_op jit(solution)/shard_map/ppermute | solution.py:528
  11.5 4.1 %collective-permute-start.1 = (f32[12,8,128]{2,1,0:T(8,128)S(1)}, f32[12,8,128]{2,1,0:T(8,128)S(1)}, u32[]{:S(2)}, u32[]{:S(2)}) collective-permute-start(f32[12,8,128]{2,1,0:T(8,128)S(1)} %get-tuple-element.28), channel_id=1, source_target_pairs={{0,120},{8,0},{16,8},{24,16},{32,24},{40,32},{48,40},{56,48},{64,5... | collective-permute-start | bytes 147464 | tf_op jit(solution)/shard_map/ppermute | solution.py:528
  15.8 7.0 %collective-permute-start.3 = (f32[8,8,128]{2,1,0:T(8,128)S(1)}, f32[8,8,128]{2,1,0:T(8,128)S(1)}, u32[]{:S(2)}, u32[]{:S(2)}) collective-permute-start(f32[8,8,128]{2,1,0:T(8,128)S(1)} %get-tuple-element.38), channel_id=1, source_target_pairs={{0,8},{8,16},{16,24},{24,32},{32,40},{40,48},{48,56},{56,64},{64,7... | collective-permute-start | bytes 98312 | tf_op jit(solution)/shard_map/ppermute | solution.py:528
  23.2 6.4 %collective-permute-start.8 = (f32[2,3,3,8,128]{4,3,2,1,0:T(8,128)S(1)}, f32[2,3,3,8,128]{4,3,2,1,0:T(8,128)S(1)}, u32[]{:S(2)}, u32[]{:S(2)}) collective-permute-start(f32[2,3,3,8,128]{4,3,2,1,0:T(8,128)S(1)} %get-tuple-element.39.after_ref.s0_ref), channel_id=1, source_target_pairs={{0,1},{1,2},{2,3},{3,0},{4,5},{5,6},{6,7},{7,4},{8,9},{9,10},{10,1... | collective-permute-start | bytes 221192 | tf_op jit(solution)/shard_map/ppermute | solution.py:533
  23.3 6.3 %collective-permute-start.7 = (f32[2,3,3,8,128]{4,3,2,1,0:T(8,128)S(1)}, f32[2,3,3,8,128]{4,3,2,1,0:T(8,128)S(1)}, u32[]{:S(2)}, u32[]{:S(2)}) collective-permute-start(f32[2,3,3,8,128]{4,3,2,1,0:T(8,128)S(1)} %get-tuple-element.39.after_ref.s0_ref), channel_id=1, source_target_pairs={{0,2},{1,3},{2,0},{3,1},{4,6},{5,7},{6,4},{7,5},{8,10},{9,11},{10,... | collective-permute-start | bytes 221192 | tf_op jit(solution)/shard_map/ppermute | solution.py:533
  24.9 5.6 %collective-permute-start.6 = (f32[2,3,3,8,128]{4,3,2,1,0:T(8,128)S(1)}, f32[2,3,3,8,128]{4,3,2,1,0:T(8,128)S(1)}, u32[]{:S(2)}, u32[]{:S(2)}) collective-permute-start(f32[2,3,3,8,128]{4,3,2,1,0:T(8,128)S(1)} %get-tuple-element.39.after_ref.s0_ref), channel_id=1, source_target_pairs={{0,3},{1,0},{2,1},{3,2},{4,7},{5,4},{6,5},{7,6},{8,11},{9,8},{10,9... | collective-permute-start | bytes 221192 | tf_op jit(solution)/shard_map/ppermute | solution.py:533
  26.5 11.6 %collective-permute-start.5 = (f32[24,8,128]{2,1,0:T(8,128)S(1)}, f32[24,8,128]{2,1,0:T(8,128)S(1)}, u32[]{:S(2)}, u32[]{:S(2)}) collective-permute-start(f32[24,8,128]{2,1,0:T(8,128)S(1)} %get-tuple-element.41), channel_id=1, source_target_pairs={{0,1},{1,2},{2,3},{3,4},{4,5},{5,6},{6,7},{7,0},{8,9},{9,10},{10,1... | collective-permute-start | bytes 294920 | tf_op jit(solution)/shard_map/ppermute | solution.py:528
  30.6 9.3 %collective-permute-start.9 = (f32[2,3,3,8,128]{4,3,2,1,0:T(8,128)S(1)}, f32[2,3,3,8,128]{4,3,2,1,0:T(8,128)S(1)}, u32[]{:S(2)}, u32[]{:S(2)}) collective-permute-start(f32[2,3,3,8,128]{4,3,2,1,0:T(8,128)S(1)} %get-tuple-element.47), channel_id=1, source_target_pairs={{0,4},{1,5},{2,6},{3,7},{4,0},{5,1},{6,2},{7,3},{8,12},{9,13},{10,... | collective-permute-start | bytes 221192 | tf_op jit(solution)/shard_map/ppermute | solution.py:528
  30.8 7.3 %collective-permute-start.4 = (f32[16,8,128]{2,1,0:T(8,128)S(1)}, f32[16,8,128]{2,1,0:T(8,128)S(1)}, u32[]{:S(2)}, u32[]{:S(2)}) collective-permute-start(f32[16,8,128]{2,1,0:T(8,128)S(1)} %get-tuple-element.40), channel_id=1, source_target_pairs={{0,8},{8,16},{16,24},{24,32},{32,40},{40,48},{48,56},{56,64},{64,7... | collective-permute-start | bytes 196616 | tf_op jit(solution)/shard_map/ppermute | solution.py:528
where the time goes:
time: 40.9 us; the launch traced here: 40.6 us
  waiting for transfers between devices  16 us (39%)
  starting transfers between devices  14.9 us (36%)
  Pallas kernels  8.99 us (22%)
  between operations  0.74 us (2%)
    ppermute x7, waiting for transfers between devices, from_ahead(): return lax.ppermute(x, axis, [(i, (i - k) % n) for i in range(n)])  12.9 us
    ppermute x7, starting transfers between devices, from_ahead(): return lax.ppermute(x, axis, [(i, (i - k) % n) for i in range(n)])  11.6 us
    pallas_call x10, Pallas kernels, call(): pl.pallas_call(kernel, out_shape=shapes, in_specs=[spec(k) for k, _ in ar...  8.99 us
    ppermute x3, starting transfers between devices, in_row(): lax.ppermute(x, 'tm', [(i, i // ROW * ROW + (i - k) % ROW) for i in range...  3.3 us
    ppermute x3, waiting for transfers between devices, in_row(): lax.ppermute(x, 'tm', [(i, i // ROW * ROW + (i - k) % ROW) for i in range...  3.11 us
  transfers between devices with their start and end apart: 10, of which 4 were waited for; matrix products, arithmetic and copies ran while one was open for 0% of the time, Pallas kernels for 16%

commit v1 on v0

--- a/solution.py
+++ b/solution.py
@@ -247,21 +247,32 @@
     accumulate(r_ref, 3, t, [down_z(v, m) for v in b], -1)
 
 
-def inner_kernel(u_ref, c_ref, r_ref):
+def flat_kernel(u_ref, c_ref, r_ref):
     link = links(tiles(u_ref, (4, 2, 3, 3, 4)))
     m = masks()
     c_ref[...] = jnp.zeros_like(c_ref)
     r_ref[...] = jnp.zeros_like(r_ref)
 
-    def spatial(t, carry):
-        ux, uy, uz = link(0, t), link(1, t), link(2, t)
+    def body(t, carry):
+        ux, uy = link(0, t), link(1, t)
         a, b = plane(ux, uy, on_mat(ux, lambda v: shift_y(v, m, True)), on_mat(uy, lambda v: shift_x(v, m, True)))
         accumulate(c_ref, 1, t, a)
         accumulate(c_ref, 0, t, b, -1)
         accumulate(r_ref, 0, t, [shift_y(v, m, False) for v in a])
         accumulate(r_ref, 1, t, [shift_x(v, m, False) for v in b], -1)
-        side_z(c_ref, r_ref, 0, shift_x, m, t, ux, uz)
-        side_z(c_ref, r_ref, 1, shift_y, m, t, uy, uz)
+        return carry
+
+    lax.fori_loop(0, 4, body, 0)
+
+
+def inner_kernel(u_ref, c_in, r_in, after_ref, c_ref, r_ref):
+    link = links(tiles(u_ref, (4, 2, 3, 3, 4)))
+    m = masks()
+
+    def spatial(t, carry):
+        uz = link(2, t)
+        side_z(c_ref, r_ref, 0, shift_x, m, t, link(0, t), uz)
+        side_z(c_ref, r_ref, 1, shift_y, m, t, link(1, t), uz)
         return carry
 
     lax.fori_loop(0, 4, spatial, 0)
@@ -548,9 +559,10 @@
     ht = ("v", from_ahead(st, "tm", 1))
     hzxy = ("v", from_ahead(szxy, "space", 1))
     acc = [("v", (4, 8, 4, 8, 128)), ("v", (4, 8, 5, 8, 128))]
-    c, r = call(inner_kernel, acc, [u], us=4.0)
+    c, r = call(flat_kernel, acc, [u], us=1.0)
     fzt, ab, uz4 = call(edge_kernel, [packed(8), packed(16), mat18], [u, ht, hzt, ("v", c)], [VMEM((2, 3, 3, 8, 128), F32)], us=0.3)
     fzt = ("v", from_ahead(fzt, "space", -1))
+    c, r = call(inner_kernel, acc, [u, ("v", c), ("v", r), ("v", ab)], (), {1: 0, 2: 1}, us=3.0)
     c, r, f3, ft = call(
         middle_kernel,
         [*acc, ("v", (8, 4, 8, 128)), packed(24)],

time: 40.9 us -> 40 us (0.978)
  waiting for transfers between devices: 16 us -> 14.7 us
    ppermute x7, waiting for transfers between devices: 12.9 us -> 11.6 us  [from_ahead(): return lax.ppermute(x, axis, [(i, (i - k) % n) for i in range(n)])]
    pallas_call x10 -> x11, Pallas kernels: 8.99 us -> 9.35 us  [call(): pl.pallas_call(kernel, out_shape=shapes, in_specs=[spec(k) for k, _ in ar...]
  transfers between devices with their start and end apart: 10 -> 10, of which waited for: 4 -> 5; matrix products, arithmetic and copies ran while one was open for 0% -> 0% of each run, Pallas kernels for 16% -> 17%
where the time goes in v1:
time: 40 us; the launch traced here: 39.6 us
  starting transfers between devices  14.9 us (37%)
  waiting for transfers between devices  14.7 us (37%)
  Pallas kernels  9.35 us (23%)
  between operations  0.73 us (2%)
    ppermute x7, starting transfers between devices, from_ahead(): return lax.ppermute(x, axis, [(i, (i - k) % n) for i in range(n)])  11.6 us
    ppermute x7, waiting for transfers between devices, from_ahead(): return lax.ppermute(x, axis, [(i, (i - k) % n) for i in range(n)])  11.6 us
    pallas_call x11, Pallas kernels, call(): pl.pallas_call(kernel, out_shape=shapes, in_specs=[spec(k) for k, _ in ar...  9.35 us
    ppermute x3, starting transfers between devices, in_row(): lax.ppermute(x, 'tm', [(i, i // ROW * ROW + (i - k) % ROW) for i in range...  3.3 us
    ppermute x3, waiting for transfers between devices, in_row(): lax.ppermute(x, 'tm', [(i, i // ROW * ROW + (i - k) % ROW) for i in range...  3.11 us
  transfers between devices with their start and end apart: 10, of which 5 were waited for; matrix products, arithmetic and copies ran while one was open for 0% of the time, Pallas kernels for 17%

profile of v1, /device:TPU:0, one launch (start us, length us, event | category | flops | bytes accessed | tf_op | source)
XLA Modules:
  0.0 39.6 jit_solution(697197857133705556)
XLA Ops:
  0.6 1.4 %shard_map.38 = (f32[4,2,3,3,4,2,4,128]{7,6,5,4,3,2,1,0:T(4,128)S(1)}, f32[36,8,128]{2,1,0:T(8,128)S(1)}, f32[12,8,128]{2,1,0:T(8,128)S(1)}, f32[24,8,128]{2,1,0:T(8,128)S(1)}) custom-call(f32[4,2,3,3,4,4,256]{6,5,4,3,2,1,0:T(4,128)} %u_hbm.1), custom_call_target="tpu_custom_call" | custom-call | flops 1000000 | bytes 3000000 | tf_op jit(solution)/shard_map/pallas_call | solution.py:525
  2.0 4.0 %collective-permute-start = (f32[36,8,128]{2,1,0:T(8,128)S(1)}, f32[36,8,128]{2,1,0:T(8,128)S(1)}, u32[]{:S(2)}, u32[]{:S(2)}) collective-permute-start(f32[36,8,128]{2,1,0:T(8,128)S(1)} %get-tuple-element.29), channel_id=1, source_target_pairs={{0,7},{1,0},{2,1},{3,2},{4,3},{5,4},{6,5},{7,6},{8,15},{9,8},{10,9... | collective-permute-start | bytes 442376 | tf_op jit(solution)/shard_map/ppermute | solution.py:539
  6.0 5.5 %collective-permute-start.2 = (f32[24,8,128]{2,1,0:T(8,128)S(1)}, f32[24,8,128]{2,1,0:T(8,128)S(1)}, u32[]{:S(2)}, u32[]{:S(2)}) collective-permute-start(f32[24,8,128]{2,1,0:T(8,128)S(1)} %get-tuple-element.39), channel_id=1, source_target_pairs={{0,120},{8,0},{16,8},{24,16},{32,24},{40,32},{48,40},{56,48},{64,5... | collective-permute-start | bytes 294920 | tf_op jit(solution)/shard_map/ppermute | solution.py:539
  11.5 1.0 %collective-permute-start.1 = (f32[12,8,128]{2,1,0:T(8,128)S(1)}, f32[12,8,128]{2,1,0:T(8,128)S(1)}, u32[]{:S(2)}, u32[]{:S(2)}) collective-permute-start(f32[12,8,128]{2,1,0:T(8,128)S(1)} %get-tuple-element.30), channel_id=1, source_target_pairs={{0,120},{8,0},{16,8},{24,16},{32,24},{40,32},{48,40},{56,48},{64,5... | collective-permute-start | bytes 147464 | tf_op jit(solution)/shard_map/ppermute | solution.py:539
  12.5 1.1 %shard_map.39 = (f32[4,8,4,8,128]{4,3,2,1,0:T(8,128)S(1)}, f32[4,8,5,8,128]{4,3,2,1,0:T(8,128)S(1)}) custom-call(f32[4,2,3,3,4,2,4,128]{7,6,5,4,3,2,1,0:T(4,128)S(1)} %get-tuple-element.28.u_ref), custom_call_target="tpu_custom_call" | custom-call | flops 1000000 | bytes 3000000 | tf_op jit(solution)/shard_map/pallas_call | solution.py:525
  13.6 1.0 %collective-permute-done.1.hzt_ref = f32[12,8,128]{2,1,0:T(8,128)S(1)} collective-permute-done((f32[12,8,128]{2,1,0:T(8,128)S(1)}, f32[12,8,128]{2,1,0:T(8,128)S(1)}, u32[]{:S(2)}, u32[]{:S(2)}) %collective-permute-start.1) | collective-permute-done | bytes 49184 | tf_op jit(solution)/shard_map/ppermute | solution.py:539
  14.5 0.0 collective-permute-done.ht_ref
  14.6 0.1 shard_map.40
  14.7 0.1 collective-permute-start.3
  14.8 2.4 %shard_map.41 = (f32[4,8,4,8,128]{4,3,2,1,0:T(8,128)S(1)}, f32[4,8,5,8,128]{4,3,2,1,0:T(8,128)S(1)}) custom-call(f32[4,2,3,3,4,2,4,128]{7,6,5,4,3,2,1,0:T(4,128)S(1)} %get-tuple-element.28.u_ref, f32[4,8,4,8,128]{4,3,2,1,0:T(8,128)S(1)} %get-tuple-element.31.after_ref.c_in, ...), custom_call_target="tpu_custom_call", output_to_operand_aliasing={{0}: (1, {}), {1}: (2, {})} | custom-call | flops 3000000 | bytes 9000000 | tf_op jit(solution)/shard_map/pallas_call | solution.py:525
  17.2 0.6 %shard_map.42 = (f32[4,8,4,8,128]{4,3,2,1,0:T(8,128)S(1)}, f32[4,8,5,8,128]{4,3,2,1,0:T(8,128)S(1)}, f32[8,4,8,128]{3,2,1,0:T(8,128)S(1)}, f32[24,8,128]{2,1,0:T(8,128)S(1)}) custom-call(f32[4,2,3,3,4,2,4,128]{7,6,5,4,3,2,1,0:T(4,128)S(1)} %get-tuple-element.28.u_ref, ...), custom_call_target="tpu_custom_call", output_to_operand_aliasing={{0}: (4, {}), {1}: (5, {})} | custom-call | flops 1000000 | bytes 3000000 | tf_op jit(solution)/shard_map/pallas_call | solution.py:525
  17.8 0.0 collective-permute-done.2.hzxy_ref
  17.8 0.4 shard_map.43
  18.2 3.7 %collective-permute-done.3.fz_ref = f32[8,8,128]{2,1,0:T(8,128)S(1)} collective-permute-done((f32[8,8,128]{2,1,0:T(8,128)S(1)}, f32[8,8,128]{2,1,0:T(8,128)S(1)}, u32[]{:S(2)}, u32[]{:S(2)}) %collective-permute-start.3) | collective-permute-done | bytes 32800 | tf_op jit(solution)/shard_map/ppermute | solution.py:539
  21.9 0.4 shard_map.44
  22.3 0.1 collective-permute-start.8
  22.3 1.2 %collective-permute-start.7 = (f32[2,3,3,8,128]{4,3,2,1,0:T(8,128)S(1)}, f32[2,3,3,8,128]{4,3,2,1,0:T(8,128)S(1)}, u32[]{:S(2)}, u32[]{:S(2)}) collective-permute-start(f32[2,3,3,8,128]{4,3,2,1,0:T(8,128)S(1)} %get-tuple-element.43.after_ref.s0_ref), channel_id=1, source_target_pairs={{0,2},{1,3},{2,0},{3,1},{4,6},{5,7},{6,4},{7,5},{8,10},{9,11},{10,... | collective-permute-start | bytes 221192 | tf_op jit(solution)/shard_map/ppermute | solution.py:544
  23.5 2.0 %collective-permute-start.6 = (f32[2,3,3,8,128]{4,3,2,1,0:T(8,128)S(1)}, f32[2,3,3,8,128]{4,3,2,1,0:T(8,128)S(1)}, u32[]{:S(2)}, u32[]{:S(2)}) collective-permute-start(f32[2,3,3,8,128]{4,3,2,1,0:T(8,128)S(1)} %get-tuple-element.43.after_ref.s0_ref), channel_id=1, source_target_pairs={{0,3},{1,0},{2,1},{3,2},{4,7},{5,4},{6,5},{7,6},{8,11},{9,8},{10,9... | collective-permute-start | bytes 221192 | tf_op jit(solution)/shard_map/ppermute | solution.py:544
  25.6 0.9 %collective-permute-start.5 = (f32[24,8,128]{2,1,0:T(8,128)S(1)}, f32[24,8,128]{2,1,0:T(8,128)S(1)}, u32[]{:S(2)}, u32[]{:S(2)}) collective-permute-start(f32[24,8,128]{2,1,0:T(8,128)S(1)} %get-tuple-element.45), channel_id=1, source_target_pairs={{0,1},{1,2},{2,3},{3,4},{4,5},{5,6},{6,7},{7,0},{8,9},{9,10},{10,1... | collective-permute-start | bytes 294920 | tf_op jit(solution)/shard_map/ppermute | solution.py:539
  26.4 2.3 %collective-permute-done.8.s3_ref = f32[2,3,3,8,128]{4,3,2,1,0:T(8,128)S(1)} collective-permute-done((f32[2,3,3,8,128]{4,3,2,1,0:T(8,128)S(1)}, f32[2,3,3,8,128]{4,3,2,1,0:T(8,128)S(1)}, u32[]{:S(2)}, u32[]{:S(2)}) %collective-permute-start.8) | collective-permute-done | bytes 73760 | tf_op jit(solution)/shard_map/ppermute | solution.py:544
  28.7 0.0 collective-permute-done.7.s2_ref
  28.7 0.9 %collective-permute-done.6.s1_ref = f32[2,3,3,8,128]{4,3,2,1,0:T(8,128)S(1)} collective-permute-done((f32[2,3,3,8,128]{4,3,2,1,0:T(8,128)S(1)}, f32[2,3,3,8,128]{4,3,2,1,0:T(8,128)S(1)}, u32[]{:S(2)}, u32[]{:S(2)}) %collective-permute-start.6) | collective-permute-done | bytes 73760 | tf_op jit(solution)/shard_map/ppermute | solution.py:544
  29.5 0.1 shard_map.47
  29.6 0.2 collective-permute-start.9
  29.9 0.0 collective-permute-start.4
  29.9 0.5 %shard_map.45.f_ref = f32[3,8,4,8,128]{4,3,2,1,0:T(8,128)S(1)} custom-call(f32[4,2,3,3,4,2,4,128]{7,6,5,4,3,2,1,0:T(4,128)S(1)} %get-tuple-element.28.u_ref, f32[4,8,4,8,128]{4,3,2,1,0:T(8,128)S(1)} %get-tuple-element.37.c_ref, f32[4,8,5,8,128]{4,3,2,1,0:T(8,128)S(1)} %get-tuple-element.38.r_ref, f32[32,8,128]{2,1,0:T(8,128)S(1)} %get-tuple-element.41.after_ref.p_ref, ...), custom_call_target="tpu_custom_call" | custom-call | flops 1000000 | bytes 3000000 | tf_op jit(solution)/shard_map/pallas_call | solution.py:525
  30.3 6.8 %collective-permute-done.4.fz_ref = f32[16,8,128]{2,1,0:T(8,128)S(1)} collective-permute-done((f32[16,8,128]{2,1,0:T(8,128)S(1)}, f32[16,8,128]{2,1,0:T(8,128)S(1)}, u32[]{:S(2)}, u32[]{:S(2)}) %collective-permute-start.4) | collective-permute-done | bytes 65568 | tf_op jit(solution)/shard_map/ppermute | solution.py:539
  37.2 0.0 collective-permute-done.5.ft_ref
  37.2 1.7 %shard_map.46 = (f32[4,2,3,3,4,4,256]{6,5,4,3,2,1,0:T(4,128)}, f32[4,2,3,3,4,4,256]{6,5,4,3,2,1,0:T(4,128)}) custom-call(f32[4,2,3,3,4,2,4,128]{7,6,5,4,3,2,1,0:T(4,128)S(1)} %get-tuple-element.28.u_ref, f32[3,8,4,8,128]{4,3,2,1,0:T(8,128)S(1)} %shard_map.45.f_ref, f32[16,8,128]{2,1,0:T(8,128)S(1)} %collective-permute-done.4.fz_ref, ...), custom_call_target="tpu_custom_call" | custom-call | flops 3000000 | bytes 9000000 | tf_op jit(solution)/shard_map/pallas_call | solution.py:525
  38.9 0.0 collective-permute-done.9.row_ref
  38.9 0.7 %shard_map.48 = f32[2,3,3,1,4,256]{5,4,3,2,1,0:T(4,128)} custom-call(f32[2,3,3,8,128]{4,3,2,1,0:T(8,128)S(1)} %get-tuple-element.50.head_ref, f32[2,3,3,8,128]{4,3,2,1,0:T(8,128)S(1)} %collective-permute-done.9.row_ref, f32[2,3,3,8,128]{4,3,2,1,0:T(8,128)S(1)} %get-tuple-element.52.tail_ref), custom_call_target="tpu_custom_call" | custom-call | flops 1000000 | bytes 3000000 | tf_op jit(solution)/shard_map/pallas_call | solution.py:525
Async XLA Ops:
  2.0 12.5 %collective-permute-start = (f32[36,8,128]{2,1,0:T(8,128)S(1)}, f32[36,8,128]{2,1,0:T(8,128)S(1)}, u32[]{:S(2)}, u32[]{:S(2)}) collective-permute-start(f32[36,8,128]{2,1,0:T(8,128)S(1)} %get-tuple-element.29), channel_id=1, source_target_pairs={{0,7},{1,0},{2,1},{3,2},{4,3},{5,4},{6,5},{7,6},{8,15},{9,8},{10,9... | collective-permute-start | bytes 442376 | tf_op jit(solution)/shard_map/ppermute | solution.py:539
  6.0 11.8 %collective-permute-start.2 = (f32[24,8,128]{2,1,0:T(8,128)S(1)}, f32[24,8,128]{2,1,0:T(8,128)S(1)}, u32[]{:S(2)}, u32[]{:S(2)}) collective-permute-start(f32[24,8,128]{2,1,0:T(8,128)S(1)} %get-tuple-element.39), channel_id=1, source_target_pairs={{0,120},{8,0},{16,8},{24,16},{32,24},{40,32},{48,40},{56,48},{64,5... | collective-permute-start | bytes 294920 | tf_op jit(solution)/shard_map/ppermute | solution.py:539
  11.5 3.0 %collective-permute-start.1 = (f32[12,8,128]{2,1,0:T(8,128)S(1)}, f32[12,8,128]{2,1,0:T(8,128)S(1)}, u32[]{:S(2)}, u32[]{:S(2)}) collective-permute-start(f32[12,8,128]{2,1,0:T(8,128)S(1)} %get-tuple-element.30), channel_id=1, source_target_pairs={{0,120},{8,0},{16,8},{24,16},{32,24},{40,32},{48,40},{56,48},{64,5... | collective-permute-start | bytes 147464 | tf_op jit(solution)/shard_map/ppermute | solution.py:539
  14.7 7.2 %collective-permute-start.3 = (f32[8,8,128]{2,1,0:T(8,128)S(1)}, f32[8,8,128]{2,1,0:T(8,128)S(1)}, u32[]{:S(2)}, u32[]{:S(2)}) collective-permute-start(f32[8,8,128]{2,1,0:T(8,128)S(1)} %get-tuple-element.42), channel_id=1, source_target_pairs={{0,8},{8,16},{16,24},{24,32},{32,40},{40,48},{48,56},{56,64},{64,7... | collective-permute-start | bytes 98312 | tf_op jit(solution)/shard_map/ppermute | solution.py:539
  22.3 6.4 %collective-permute-start.8 = (f32[2,3,3,8,128]{4,3,2,1,0:T(8,128)S(1)}, f32[2,3,3,8,128]{4,3,2,1,0:T(8,128)S(1)}, u32[]{:S(2)}, u32[]{:S(2)}) collective-permute-start(f32[2,3,3,8,128]{4,3,2,1,0:T(8,128)S(1)} %get-tuple-element.43.after_ref.s0_ref), channel_id=1, source_target_pairs={{0,1},{1,2},{2,3},{3,0},{4,5},{5,6},{6,7},{7,4},{8,9},{9,10},{10,1... | collective-permute-start | bytes 221192 | tf_op jit(solution)/shard_map/ppermute | solution.py:544
  22.3 6.3 %collective-permute-start.7 = (f32[2,3,3,8,128]{4,3,2,1,0:T(8,128)S(1)}, f32[2,3,3,8,128]{4,3,2,1,0:T(8,128)S(1)}, u32[]{:S(2)}, u32[]{:S(2)}) collective-permute-start(f32[2,3,3,8,128]{4,3,2,1,0:T(8,128)S(1)} %get-tuple-element.43.after_ref.s0_ref), channel_id=1, source_target_pairs={{0,2},{1,3},{2,0},{3,1},{4,6},{5,7},{6,4},{7,5},{8,10},{9,11},{10,... | collective-permute-start | bytes 221192 | tf_op jit(solution)/shard_map/ppermute | solution.py:544
  23.5 6.0 %collective-permute-start.6 = (f32[2,3,3,8,128]{4,3,2,1,0:T(8,128)S(1)}, f32[2,3,3,8,128]{4,3,2,1,0:T(8,128)S(1)}, u32[]{:S(2)}, u32[]{:S(2)}) collective-permute-start(f32[2,3,3,8,128]{4,3,2,1,0:T(8,128)S(1)} %get-tuple-element.43.after_ref.s0_ref), channel_id=1, source_target_pairs={{0,3},{1,0},{2,1},{3,2},{4,7},{5,4},{6,5},{7,6},{8,11},{9,8},{10,9... | collective-permute-start | bytes 221192 | tf_op jit(solution)/shard_map/ppermute | solution.py:544
  25.6 11.6 %collective-permute-start.5 = (f32[24,8,128]{2,1,0:T(8,128)S(1)}, f32[24,8,128]{2,1,0:T(8,128)S(1)}, u32[]{:S(2)}, u32[]{:S(2)}) collective-permute-start(f32[24,8,128]{2,1,0:T(8,128)S(1)} %get-tuple-element.45), channel_id=1, source_target_pairs={{0,1},{1,2},{2,3},{3,4},{4,5},{5,6},{6,7},{7,0},{8,9},{9,10},{10,1... | collective-permute-start | bytes 294920 | tf_op jit(solution)/shard_map/ppermute | solution.py:539
  29.6 9.3 %collective-permute-start.9 = (f32[2,3,3,8,128]{4,3,2,1,0:T(8,128)S(1)}, f32[2,3,3,8,128]{4,3,2,1,0:T(8,128)S(1)}, u32[]{:S(2)}, u32[]{:S(2)}) collective-permute-start(f32[2,3,3,8,128]{4,3,2,1,0:T(8,128)S(1)} %get-tuple-element.51), channel_id=1, source_target_pairs={{0,4},{1,5},{2,6},{3,7},{4,0},{5,1},{6,2},{7,3},{8,12},{9,13},{10,... | collective-permute-start | bytes 221192 | tf_op jit(solution)/shard_map/ppermute | solution.py:539
  29.9 7.3 %collective-permute-start.4 = (f32[16,8,128]{2,1,0:T(8,128)S(1)}, f32[16,8,128]{2,1,0:T(8,128)S(1)}, u32[]{:S(2)}, u32[]{:S(2)}) collective-permute-start(f32[16,8,128]{2,1,0:T(8,128)S(1)} %get-tuple-element.44), channel_id=1, source_target_pairs={{0,8},{8,16},{16,24},{24,32},{32,40},{40,48},{48,56},{56,64},{64,7... | collective-permute-start | bytes 196616 | tf_op jit(solution)/shard_map/ppermute | solution.py:539

commit v2 on v0

--- a/solution.py
+++ b/solution.py
@@ -166,43 +166,58 @@
     return twice_ta(g, d), twice_ta(d, g)
 
 
+def corner_loop(u_mu, u_nu, mu_up, nu_up, at_nu):
+    d = product(u_mu, u_nu, ha=True)
+    g = product(mu_up, nu_up, hb=True)
+    return twice_ta(g, d) if at_nu else twice_ta(d, g)
+
+
 def unpack_rows(ref, base):
     m = [[(ref[base * 12 + i * 3 + j], ref[base * 12 + 6 + i * 3 + j]) for j in range(3)] for i in range(2)]
+    return m + [third_row(m)]
+
+
+def third_row(m):
     third = []
     for k in range(3):
         a, b = (k + 1) % 3, (k + 2) % 3
         r1, i1 = entry([(m[0][a], False, m[1][b], False)])
         r2, i2 = entry([(m[0][b], False, m[1][a], False)])
         third.append((r1 - r2, i2 - i1))
-    return m + [third]
+    return third
 
 
 def tiles(ref, shape):
     return ref.reshape(*shape, 8, 128)
 
 
-def load_kernel(u_hbm, u_ref, st_ref, szt_ref, szxy_ref, sem):
+FIRST = pl.ds(0, 8, stride=4)
+LAST = pl.ds(3, 8, stride=4)
+
+
+def load_kernel(u_hbm, u_ref, st_ref, low_ref, high_ref, corner_ref, sem):
     copies = {}
-    for d in (3, 0, 1, 2):
+    for d in range(4):
         for h in range(2):
             src = u_hbm.at[d, :, :, :, :, :, pl.ds(128 * h, 128)]
             copies[d, h] = pltpu.make_async_copy(src, u_ref.at[d, :, :, :, :, h], sem.at[d, h])
             copies[d, h].start()
     u = tiles(u_ref, (4, 2, 3, 3, 4))
     rows = u_ref.reshape(4, 2, 3, 3, 32, 128)
-    for d in (3, 0, 1, 2):
+    for d in range(4):
         for h in range(2):
             copies[d, h].wait()
         for p in range(2):
             for i in range(2):
                 for j in range(3):
                     k = p * 6 + i * 3 + j
+                    high_ref[d * 12 + k] = rows[d, p, i, j, LAST, :]
                     if d < 3:
                         st_ref[d * 12 + k] = u[d, p, i, j, 0]
-                    if d < 2:
-                        szxy_ref[d * 12 + k] = rows[d, p, i, j, pl.ds(0, 8, stride=4), :]
-                    if d == 3:
-                        szt_ref[k] = rows[d, p, i, j, pl.ds(0, 8, stride=4), :]
+                    if d != 2:
+                        low_ref[min(d, 2) * 12 + k] = rows[d, p, i, j, FIRST, :]
+                    if d == 2:
+                        corner_ref[pl.ds(2 * k, 2), :] = rows[d, p, i, j, pl.ds(3, 2, stride=4), :]
 
 
 def accumulate(ref, mu, t, vals, sign=1):
@@ -247,13 +262,26 @@
     accumulate(r_ref, 3, t, [down_z(v, m) for v in b], -1)
 
 
-def inner_kernel(u_ref, c_ref, r_ref):
+def steep_kernel(u_ref, c_ref, r_ref):
     link = links(tiles(u_ref, (4, 2, 3, 3, 4)))
     m = masks()
     c_ref[...] = jnp.zeros_like(c_ref)
     r_ref[...] = jnp.zeros_like(r_ref)
 
-    def spatial(t, carry):
+    def body(t, carry):
+        for mu, shift in ((0, shift_x), (1, shift_y)):
+            side_time(c_ref, r_ref, mu, shift, m, t, link(mu, t), link(3, t), link(mu, t + 1))
+        zt_inside(c_ref, r_ref, m, t, link(2, t), link(3, t), link(2, t + 1))
+        return carry
+
+    lax.fori_loop(0, 3, body, 0)
+
+
+def flat_kernel(u_ref, c_in, r_in, after_ref, c_ref, r_ref):
+    link = links(tiles(u_ref, (4, 2, 3, 3, 4)))
+    m = masks()
+
+    def body(t, carry):
         ux, uy, uz = link(0, t), link(1, t), link(2, t)
         a, b = plane(ux, uy, on_mat(ux, lambda v: shift_y(v, m, True)), on_mat(uy, lambda v: shift_x(v, m, True)))
         accumulate(c_ref, 1, t, a)
@@ -264,15 +292,7 @@
         side_z(c_ref, r_ref, 1, shift_y, m, t, uy, uz)
         return carry
 
-    lax.fori_loop(0, 4, spatial, 0)
-
-    def timelike(t, carry):
-        for mu, shift in ((0, shift_x), (1, shift_y)):
-            side_time(c_ref, r_ref, mu, shift, m, t, link(mu, t), link(3, t), link(mu, t + 1))
-        zt_inside(c_ref, r_ref, m, t, link(2, t), link(3, t), link(2, t + 1))
-        return carry
-
-    lax.fori_loop(0, 3, timelike, 0)
+    lax.fori_loop(0, 4, body, 0)
 
 
 def side_time(c_ref, r_ref, mu, shift, m, t, u_mu, u_t, mu_up):
@@ -283,27 +303,6 @@
     accumulate(r_ref, 3, t, [shift(v, m, False) for v in b], -1)
 
 
-LAST = pl.ds(3, 8, stride=4)
-
-
-def edge_kernel(u_ref, ht_ref, hzt_ref, after_ref, fzt_ref, ab_ref, uz4_ref, pk_ref):
-    rows = u_ref.reshape(4, 2, 3, 3, 32, 128)
-    above = unpack_rows(ht_ref, 2)
-    for p in range(2):
-        for i in range(3):
-            for j in range(3):
-                uz4_ref[p, i, j] = above[i][j][p]
-                pk_ref[p, i, j, pl.ds(0, 6), :] = rows[2, p, i, j, pl.ds(11, 6, stride=4), :]
-                pk_ref[p, i, j, pl.ds(6, 2), :] = uz4_ref[p, i, j, pl.ds(3, 2, stride=4), :]
-    uz = mat(lambda p, i, j: rows[2, p, i, j, LAST, :])
-    ut = mat(lambda p, i, j: rows[3, p, i, j, LAST, :])
-    a, b = plane(uz, ut, mat(lambda p, i, j: pk_ref[p, i, j]), unpack_rows(hzt_ref, 0))
-    for k in range(8):
-        fzt_ref[k] = -b[k]
-        ab_ref[k] = a[k]
-        ab_ref[8 + k] = b[k]
-
-
 def expand(x_ref, n, tile, offset):
     x_ref[n] = jnp.zeros((32, 128), F32)
     x_ref[n, pl.ds(offset, 8, stride=4), :] = tile
@@ -311,33 +310,6 @@
 
 def at(t):
     return pl.ds(t * 8 if isinstance(t, int) else pl.multiple_of(t * 8, 8), 8)
-
-
-def middle_kernel(u_ref, ht_ref, uz4_ref, ab_ref, c_in, r_in, c_ref, r_ref, f_ref, ft_ref, x_ref):
-    link = links(tiles(u_ref, (4, 2, 3, 3, 4)))
-    m = masks()
-    for k in range(16):
-        expand(x_ref, k, ab_ref[k], 3)
-    for k in range(8):
-        for t in range(4):
-            a = x_ref[k, at(t), :]
-            c_ref[3, k, t] += a
-            c_ref[2, k, t] -= x_ref[8 + k, at(t), :]
-            r_ref[2, k, t + 1] += a
-    for mu, shift in ((0, shift_x), (1, shift_y)):
-        side_time(c_ref, r_ref, mu, shift, m, 3, link(mu, 3), link(3, 3), unpack_rows(ht_ref, mu))
-    zt_inside(c_ref, r_ref, m, 3, link(2, 3), link(3, 3), get18(uz4_ref))
-    for mu in range(3):
-        for k in range(8):
-            ft_ref[mu * 8 + k] = r_ref[mu, k, 4]
-
-    def body(t, carry):
-        w = transport(link(3, t), [c_ref[3, k, t] for k in range(8)])
-        for k in range(8):
-            f_ref[k, t] = w[k] + r_ref[3, k, t]
-        return carry
-
-    lax.fori_loop(0, 4, body, 0)
 
 
 def packed_shift_y(v, m, up):
@@ -346,38 +318,8 @@
     return jnp.where(m["y"] == (7 if up else 0), other, r)
 
 
-def late_edge_kernel(u_ref, hzxy_ref, after_ref, fz_ref, p_ref):
-    rows = u_ref.reshape(4, 2, 3, 3, 32, 128)
-    m = masks()
-    m["odd"] = (lax.broadcasted_iota(jnp.int32, (8, 128), 0) & 1) == 1
-    uz = mat(lambda p, i, j: rows[2, p, i, j, LAST, :])
-    for mu, shift in ((0, shift_x), (1, packed_shift_y)):
-        um = mat(lambda p, i, j: rows[mu, p, i, j, LAST, :])
-        a, b = plane(um, uz, unpack_rows(hzxy_ref, mu), on_mat(uz, lambda v: shift(v, m, True)))
-        for k in range(8):
-            fz_ref[mu * 8 + k] = a[k]
-            p_ref[mu * 8 + k] = b[k]
-            back = shift(b[k], m, False)
-            p_ref[16 + k] = a[k] if mu == 0 else p_ref[16 + k] + a[k]
-            p_ref[24 + k] = back if mu == 0 else p_ref[24 + k] + back
-
-
-def space_sum_kernel(u_ref, c_ref, r_ref, p_ref, after_ref, f_ref, x_ref):
-    link = links(tiles(u_ref, (4, 2, 3, 3, 4)))
-    for k in range(32):
-        expand(x_ref, k, p_ref[k], 3)
-
-    def body(t, carry):
-        for mu in range(3):
-            x = [x_ref[(16 if mu == 2 else mu * 8) + k, at(t), :] for k in range(8)]
-            c = [c_ref[mu, k, t] for k in range(8)]
-            w = transport(link(mu, t), [a + b if mu == 2 else a - b for a, b in zip(c, x)])
-            for k in range(8):
-                v = w[k] + r_ref[mu, k, t]
-                f_ref[mu, k, t] = v - x_ref[24 + k, at(t), :] if mu == 2 else v
-        return carry
-
-    lax.fori_loop(0, 4, body, 0)
+def packed(rows, d, part):
+    return mat(lambda p, i, j: rows[d, p, i, j, part, :])
 
 
 def finish(f, u, z_out, new_out):
@@ -406,15 +348,43 @@
     return put
 
 
-def time_kernel(u_ref, f_ref, fz_ref, after_ref, zt_ref, nt_ref, s_ref, x_ref):
+def time_kernel(u_ref, ht_ref, low_ref, high_ref, corner_ref, c_in, r_in, c_ref, r_ref, ft_ref, ab_ref, zt_ref, nt_ref, s_ref, x_ref, uz4_ref, pk_ref):
     link = links(tiles(u_ref, (4, 2, 3, 3, 4)))
+    rows = u_ref.reshape(4, 2, 3, 3, 32, 128)
     zt, nt = tiles(zt_ref, (2, 3, 3, 4)), tiles(nt_ref, (2, 3, 3, 4))
+    m = masks()
+    above = unpack_rows(ht_ref, 2)
+    for p in range(2):
+        for i in range(3):
+            for j in range(3):
+                uz4_ref[p, i, j] = above[i][j][p]
+                pk_ref[p, i, j, pl.ds(0, 6), :] = rows[2, p, i, j, pl.ds(11, 6, stride=4), :]
+                pk_ref[p, i, j, pl.ds(6, 2), :] = uz4_ref[p, i, j, pl.ds(3, 2, stride=4), :]
+    a, b = plane(packed(rows, 2, LAST), packed(rows, 3, LAST), get18(pk_ref), unpack_rows(low_ref, 2))
     for k in range(8):
-        expand(x_ref, k, fz_ref[k], 0)
+        ab_ref[k] = a[k]
+        ab_ref[8 + k] = b[k]
+        expand(x_ref, k, a[k], 3)
+    for k in range(12):
+        pk_ref[k // 6, k // 3 % 2, k % 3, pl.ds(0, 6), :] = high_ref[24 + k, pl.ds(2, 6), :]
+        pk_ref[k // 6, k // 3 % 2, k % 3, pl.ds(6, 2), :] = corner_ref[pl.ds(2 * k, 2), :]
+    up = [[(pk_ref[0, i, j], pk_ref[1, i, j]) for j in range(3)] for i in range(2)]
+    b = corner_loop(unpack_rows(high_ref, 2), unpack_rows(high_ref, 3), up + [third_row(up)], packed(rows, 3, FIRST), False)
+    for k in range(8):
+        expand(x_ref, 8 + k, b[k], 0)
+    for mu, shift in ((0, shift_x), (1, shift_y)):
+        side_time(c_ref, r_ref, mu, shift, m, 3, link(mu, 3), link(3, 3), unpack_rows(ht_ref, mu))
+    zt_inside(c_ref, r_ref, m, 3, link(2, 3), link(3, 3), get18(uz4_ref))
+    for mu in range(3):
+        for k in range(8):
+            v = r_ref[mu, k, 4]
+            ft_ref[mu * 8 + k] = v + x_ref[k, at(3), :] if mu == 2 else v
 
     def body(t, carry):
-        f = [f_ref[k, t] + x_ref[k, at(t), :] for k in range(8)]
-        finish(f, link(3, t), writer(zt, t=t), writer(nt, t=t))
+        u = link(3, t)
+        w = transport(u, [c_ref[3, k, t] + x_ref[k, at(t), :] for k in range(8)])
+        f = [w[k] + (r_ref[3, k, t] - x_ref[8 + k, at(t), :]) for k in range(8)]
+        finish(f, u, writer(zt, t=t), writer(nt, t=t))
         return carry
 
     lax.fori_loop(0, 4, body, 0)
@@ -428,23 +398,42 @@
     return [pltpu.make_async_copy(src.at[:, :, :, :, h], dst.at[d, :, :, :, :, :, pl.ds(128 * h, 128)], sem.at[h]) for h in range(2)]
 
 
-def space_kernel(u_ref, f_ref, fz_ref, ft_ref, zt_ref, nt_ref, new_hbm, z_hbm, zs_ref, ns_ref, x_ref, sem):
+def space_kernel(u_ref, low_ref, high_ref, ab_ref, ft_ref, c_ref, r_ref, zt_ref, nt_ref, new_hbm, z_hbm, zs_ref, ns_ref, x_ref, sem):
     link = links(tiles(u_ref, (4, 2, 3, 3, 4)))
+    rows = u_ref.reshape(4, 2, 3, 3, 32, 128)
     copies = out_copies(zt_ref, z_hbm, sem.at[6], 3) + out_copies(nt_ref, new_hbm, sem.at[7], 3)
     for c in copies:
         c.start()
-    for k in range(16):
-        expand(x_ref, k, fz_ref[k], 0)
-    for k in range(24):
-        f_ref[k // 8, k % 8, 0] += ft_ref[k]
-    for mu in range(3):
+    m = masks()
+    line = lax.broadcasted_iota(jnp.int32, (8, 128), 0)
+    m["odd"] = (line & 1) == 1
+    uz = packed(rows, 2, LAST)
+    uz_low = unpack_rows(high_ref, 2)
+    cz = [-ab_ref[8 + k] for k in range(8)]
+    rz = [jnp.where(line >= 2, pltpu.roll(ab_ref[k], 2, 0), 0.0) for k in range(8)]
+    for mu, shift in ((0, shift_x), (1, packed_shift_y)):
+        a, b = plane(packed(rows, mu, LAST), uz, unpack_rows(low_ref, mu), on_mat(uz, lambda v: shift(v, m, True)))
+        for k in range(8):
+            expand(x_ref, mu * 8 + k, -b[k], 3)
+        cz = [v + a[k] for k, v in enumerate(cz)]
+        rz = [v - shift(b[k], m, False) for k, v in enumerate(rz)]
+        a = corner_loop(unpack_rows(high_ref, mu), uz_low, packed(rows, mu, FIRST), on_mat(uz_low, lambda v: shift(v, m, True)), True)
+        for k in range(8):
+            expand(x_ref, 32 + mu * 8 + k, a[k], 0)
+    for k in range(8):
+        expand(x_ref, 16 + k, cz[k], 3)
+        expand(x_ref, 24 + k, rz[k], 3)
+    for mu, first in ((0, 32), (1, 40), (2, 24)):
+        for k in range(8):
+            x_ref[first + k, at(0), :] += ft_ref[mu * 8 + k]
+    for mu, first in ((0, 32), (1, 40), (2, 24)):
         zs, ns = tiles(zs_ref.at[mu], (2, 3, 3, 4)), tiles(ns_ref.at[mu], (2, 3, 3, 4))
 
         def body(t, carry):
-            f = [f_ref[mu, k, t] for k in range(8)]
-            if mu < 2:
-                f = [v + x_ref[mu * 8 + k, at(t), :] for k, v in enumerate(f)]
-            finish(f, link(mu, t), writer(zs, t=t), writer(ns, t=t))
+            u = link(mu, t)
+            w = transport(u, [c_ref[mu, k, t] + x_ref[mu * 8 + k, at(t), :] for k in range(8)])
+            f = [w[k] + (r_ref[mu, k, t] + x_ref[first + k, at(t), :]) for k in range(8)]
+            finish(f, u, writer(zs, t=t), writer(ns, t=t))
             return carry
 
         lax.fori_loop(0, 4, body, 0)
@@ -528,6 +517,12 @@
     return lax.ppermute(x, axis, [(i, (i - k) % n) for i in range(n)])
 
 
+def diagonal(x):
+    n, k = lax.axis_size("space"), lax.axis_size("tm")
+    pairs = [(i * k + j, (i + 1) % n * k + (j - 1) % k) for i in range(n) for j in range(k)]
+    return lax.ppermute(x, ("space", "tm"), pairs)
+
+
 def in_row(x, k):
     n = lax.axis_size("tm")
     return lax.ppermute(x, "tm", [(i, i // ROW * ROW + (i - k) % ROW) for i in range(n)])
@@ -539,40 +534,39 @@
     mat18 = ("v", (2, 3, 3, 8, 128))
     full = ("h", gauge_links.shape)
 
-    def packed(n):
+    def pack(n):
         return ("v", (n, 8, 128))
 
-    u, st, szt, szxy = call(load_kernel, [("v", whole), packed(36), packed(12), packed(24)], [("h", gauge_links)], [dma((4, 2))])
+    u, st, low, high, corner = call(
+        load_kernel, [("v", whole), pack(36), pack(36), pack(48), ("v", (24, 128))], [("h", gauge_links)], [dma((4, 2))]
+    )
     u = ("v", u)
-    hzt = ("v", from_ahead(szt, "space", 1))
+    high = ("v", from_ahead(high, "space", -1))
+    corner = ("v", diagonal(corner))
     ht = ("v", from_ahead(st, "tm", 1))
-    hzxy = ("v", from_ahead(szxy, "space", 1))
+    low = ("v", from_ahead(low, "space", 1))
     acc = [("v", (4, 8, 4, 8, 128)), ("v", (4, 8, 5, 8, 128))]
-    c, r = call(inner_kernel, acc, [u], us=4.0)
-    fzt, ab, uz4 = call(edge_kernel, [packed(8), packed(16), mat18], [u, ht, hzt, ("v", c)], [VMEM((2, 3, 3, 8, 128), F32)], us=0.3)
-    fzt = ("v", from_ahead(fzt, "space", -1))
-    c, r, f3, ft = call(
-        middle_kernel,
-        [*acc, ("v", (8, 4, 8, 128)), packed(24)],
-        [u, ht, ("v", uz4), ("v", ab), ("v", c), ("v", r)],
-        [VMEM((16, 32, 128), F32)],
-        {4: 0, 5: 1},
+    slices = ("v", (2, 3, 3, 4, 2, 4, 128))
+    c, r = call(steep_kernel, acc, [u], us=1.5)
+    c, r, ft, ab, zt, nt, s = call(
+        time_kernel,
+        [*acc, pack(24), pack(16), slices, slices, mat18],
+        [u, ht, low, high, corner, ("v", c), ("v", r)],
+        [VMEM((16, 32, 128), F32), VMEM((2, 3, 3, 8, 128), F32), VMEM((2, 3, 3, 8, 128), F32)],
+        {5: 0, 6: 1},
+        us=1.4,
     )
+    s1, s3, s2 = in_row(s, 1), in_row(s, 3), in_row(s, 2)
     ft = ("v", from_ahead(ft, "tm", -1))
-    fz, p = call(late_edge_kernel, [packed(16), packed(32)], [u, hzxy, ("v", f3)], us=0.5)
-    fz = ("v", from_ahead(fz, "space", -1))
-    slices = ("v", (2, 3, 3, 4, 2, 4, 128))
-    zt, nt, s = call(time_kernel, [slices, slices, mat18], [u, ("v", f3), fzt, ("v", p)], [VMEM((8, 32, 128), F32)], us=0.4)
-    s1, s3, s2 = in_row(s, 1), in_row(s, 3), in_row(s, 2)
-    (f,) = call(space_sum_kernel, [("v", (3, 8, 4, 8, 128))], [u, ("v", c), ("v", r), ("v", p), ("v", s)], [VMEM((32, 32, 128), F32)], us=1.0)
+    c, r = call(flat_kernel, acc, [u, ("v", c), ("v", r), ("v", s)], (), {1: 0, 2: 1}, us=2.0)
     head, tail, row = call(join_kernel, [mat18] * 3, [("v", s), ("v", s1), ("v", s2), ("v", s3)], us=0.1)
     row = from_ahead(row, "tm", ROW)
     stage = VMEM((3, 2, 3, 3, 4, 2, 4, 128), F32)
     new, force = call(
         space_kernel,
         [full, full],
-        [u, ("v", f), fz, ft, ("v", zt), ("v", nt)],
-        [stage, stage, VMEM((16, 32, 128), F32), dma((8, 2))],
+        [u, low, high, ("v", ab), ft, ("v", c), ("v", r), ("v", zt), ("v", nt)],
+        [stage, stage, VMEM((48, 32, 128), F32), dma((8, 2))],
         us=3.0,
     )
     (hol,) = call(

time: 40.9 us -> 34.4 us (0.84)
  waiting for transfers between devices: 16 us -> 8.77 us
  starting transfers between devices: 14.9 us -> 15.6 us
    ppermute x7 -> x5, waiting for transfers between devices: 12.9 us -> 0.01 us  [from_ahead(): return lax.ppermute(x, axis, [(i, (i - k) % n) for i in range(n)])]
    ppermute x0 -> x1, waiting for transfers between devices: none -> 6.43 us  [diagonal(): return lax.ppermute(x, ('space', 'tm'), pairs)]
    ppermute x3, waiting for transfers between devices: 3.11 us -> 2.33 us  [in_row(): lax.ppermute(x, 'tm', [(i, i // ROW * ROW + (i - k) % ROW) for i in range...]
    ppermute x7 -> x5, starting transfers between devices: 11.6 us -> 12.2 us  [from_ahead(): return lax.ppermute(x, axis, [(i, (i - k) % n) for i in range(n)])]
    pallas_call x10 -> x7, Pallas kernels: 8.99 us -> 9.14 us  [call(): pl.pallas_call(kernel, out_shape=shapes, in_specs=[spec(k) for k, _ in ar...]
  transfers between devices with their start and end apart: 10 -> 9, of which waited for: 4 -> 3; matrix products, arithmetic and copies ran while one was open for 0% -> 0% of each run, Pallas kernels for 16% -> 17%
where the time goes in v2:
time: 34.4 us; the launch traced here: 34.2 us
  starting transfers between devices  15.6 us (45%)
  Pallas kernels  9.14 us (27%)
  waiting for transfers between devices  8.77 us (25%)
  between operations  0.71 us (2%)
    ppermute x5, starting transfers between devices, from_ahead(): return lax.ppermute(x, axis, [(i, (i - k) % n) for i in range(n)])  12.2 us
    pallas_call x7, Pallas kernels, call(): pl.pallas_call(kernel, out_shape=shapes, in_specs=[spec(k) for k, _ in ar...  9.14 us
    ppermute x1, waiting for transfers between devices, diagonal(): return lax.ppermute(x, ('space', 'tm'), pairs)  6.43 us
    ppermute x3, starting transfers between devices, in_row(): lax.ppermute(x, 'tm', [(i, i // ROW * ROW + (i - k) % ROW) for i in range...  3.44 us
    ppermute x3, waiting for transfers between devices, in_row(): lax.ppermute(x, 'tm', [(i, i // ROW * ROW + (i - k) % ROW) for i in range...  2.33 us
  transfers between devices with their start and end apart: 9, of which 3 were waited for; matrix products, arithmetic and copies ran while one was open for 0% of the time, Pallas kernels for 17%

profile of v2, /device:TPU:0, one launch (start us, length us, event | category | flops | bytes accessed | tf_op | source)
XLA Modules:
  0.0 34.2 jit_solution(603213641117357003)
XLA Ops:
  0.6 1.4 %shard_map.38 = (f32[4,2,3,3,4,2,4,128]{7,6,5,4,3,2,1,0:T(4,128)S(1)}, f32[36,8,128]{2,1,0:T(8,128)S(1)}, f32[36,8,128]{2,1,0:T(8,128)S(1)}, f32[48,8,128]{2,1,0:T(8,128)S(1)}, f32[24,128]{1,0:T(8,128)S(1)}) custom-call(f32[4,2,3,3,4,4,256]{6,5,4,3,2,1,0:T(4,128)} %u_hbm.1), custom_call_target="tpu_custom_call" | custom-call | flops 1000000 | bytes 3000000 | tf_op jit(solution)/shard_map/pallas_call | solution.py:503
  2.0 0.1 collective-permute-start.1
  2.1 6.3 %collective-permute-start = (f32[36,8,128]{2,1,0:T(8,128)S(1)}, f32[36,8,128]{2,1,0:T(8,128)S(1)}, u32[]{:S(2)}, u32[]{:S(2)}) collective-permute-start(f32[36,8,128]{2,1,0:T(8,128)S(1)} %get-tuple-element.25), channel_id=1, source_target_pairs={{0,120},{8,0},{16,8},{24,16},{32,24},{40,32},{48,40},{56,48},{64,5... | collective-permute-start | bytes 442376 | tf_op jit(solution)/shard_map/ppermute | solution.py:517
  8.4 2.9 %collective-permute-start.2 = (f32[36,8,128]{2,1,0:T(8,128)S(1)}, f32[36,8,128]{2,1,0:T(8,128)S(1)}, u32[]{:S(2)}, u32[]{:S(2)}) collective-permute-start(f32[36,8,128]{2,1,0:T(8,128)S(1)} %get-tuple-element.27), channel_id=1, source_target_pairs={{0,7},{1,0},{2,1},{3,2},{4,3},{5,4},{6,5},{7,6},{8,15},{9,8},{10,9... | collective-permute-start | bytes 442376 | tf_op jit(solution)/shard_map/ppermute | solution.py:517
  11.4 0.0 collective-permute-start.3
  11.4 1.2 %shard_map.39 = (f32[4,8,4,8,128]{4,3,2,1,0:T(8,128)S(1)}, f32[4,8,5,8,128]{4,3,2,1,0:T(8,128)S(1)}) custom-call(f32[4,2,3,3,4,2,4,128]{7,6,5,4,3,2,1,0:T(4,128)S(1)} %get-tuple-element.24.u_ref), custom_call_target="tpu_custom_call" | custom-call | flops 1500000 | bytes 4500000 | tf_op jit(solution)/shard_map/pallas_call | solution.py:503
  12.6 6.4 %collective-permute-done.3.corner_ref = f32[24,128]{1,0:T(8,128)S(1)} collective-permute-done((f32[24,128]{1,0:T(8,128)S(1)}, f32[24,128]{1,0:T(8,128)S(1)}, u32[]{:S(2)}, u32[]{:S(2)}) %collective-permute-start.3) | collective-permute-done | bytes 12320 | tf_op jit(solution)/shard_map/ppermute | solution.py:523
  19.0 0.0 collective-permute-done.low_ref
  19.0 0.0 collective-permute-done.2.ht_ref
  19.0 0.0 collective-permute-done.1.high_ref
  19.0 1.1 %shard_map.40 = (f32[4,8,4,8,128]{4,3,2,1,0:T(8,128)S(1)}, f32[4,8,5,8,128]{4,3,2,1,0:T(8,128)S(1)}, f32[24,8,128]{2,1,0:T(8,128)S(1)}, f32[16,8,128]{2,1,0:T(8,...) custom-call(f32[4,2,3,3,4,2,4,128]{7,6,5,4,3,2,1,0:T(4,128)S(1)} %ge, ...), custom_call_target="tpu_custom_call", output_to_operand_aliasing={{0}: (5, {}), {1}: (6, {})} | custom-call | flops 1400000 | bytes 4200000 | tf_op jit(solution)/shard_map/pallas_call | solution.py:503
  20.1 0.1 collective-permute-start.7
  20.2 3.1 %collective-permute-start.6 = (f32[2,3,3,8,128]{4,3,2,1,0:T(8,128)S(1)}, f32[2,3,3,8,128]{4,3,2,1,0:T(8,128)S(1)}, u32[]{:S(2)}, u32[]{:S(2)}) collective-permute-start(f32[2,3,3,8,128]{4,3,2,1,0:T(8,128)S(1)} %get-tuple-element.35.after_ref.s0_ref), channel_id=1, source_target_pairs={{0,2},{1,3},{2,0},{3,1},{4,6},{5,7},{6,4},{7,5},{8,10},{9,11},{10,... | collective-permute-start | bytes 221192 | tf_op jit(solution)/shard_map/ppermute | solution.py:528
  23.3 0.2 collective-permute-start.5
  23.6 1.8 %collective-permute-start.4 = (f32[24,8,128]{2,1,0:T(8,128)S(1)}, f32[24,8,128]{2,1,0:T(8,128)S(1)}, u32[]{:S(2)}, u32[]{:S(2)}) collective-permute-start(f32[24,8,128]{2,1,0:T(8,128)S(1)} %get-tuple-element.32), channel_id=1, source_target_pairs={{0,1},{1,2},{2,3},{3,4},{4,5},{5,6},{6,7},{7,0},{8,9},{9,10},{10,1... | collective-permute-start | bytes 294920 | tf_op jit(solution)/shard_map/ppermute | solution.py:517
  25.4 2.0 %collective-permute-done.7.s3_ref = f32[2,3,3,8,128]{4,3,2,1,0:T(8,128)S(1)} collective-permute-done((f32[2,3,3,8,128]{4,3,2,1,0:T(8,128)S(1)}, f32[2,3,3,8,128]{4,3,2,1,0:T(8,128)S(1)}, u32[]{:S(2)}, u32[]{:S(2)}) %collective-permute-start.7) | collective-permute-done | bytes 73760 | tf_op jit(solution)/shard_map/ppermute | solution.py:528
  27.3 0.0 collective-permute-done.6.s2_ref
  27.3 0.4 %collective-permute-done.5.s1_ref = f32[2,3,3,8,128]{4,3,2,1,0:T(8,128)S(1)} collective-permute-done((f32[2,3,3,8,128]{4,3,2,1,0:T(8,128)S(1)}, f32[2,3,3,8,128]{4,3,2,1,0:T(8,128)S(1)}, u32[]{:S(2)}, u32[]{:S(2)}) %collective-permute-start.5) | collective-permute-done | bytes 73760 | tf_op jit(solution)/shard_map/ppermute | solution.py:528
  27.7 0.1 shard_map.43
  27.8 1.1 %collective-permute-start.8 = (f32[2,3,3,8,128]{4,3,2,1,0:T(8,128)S(1)}, f32[2,3,3,8,128]{4,3,2,1,0:T(8,128)S(1)}, u32[]{:S(2)}, u32[]{:S(2)}) collective-permute-start(f32[2,3,3,8,128]{4,3,2,1,0:T(8,128)S(1)} %get-tuple-element.43), channel_id=1, source_target_pairs={{0,4},{1,5},{2,6},{3,7},{4,0},{5,1},{6,2},{7,3},{8,12},{9,13},{10,... | collective-permute-start | bytes 221192 | tf_op jit(solution)/shard_map/ppermute | solution.py:517
  28.9 2.0 %shard_map.41 = (f32[4,8,4,8,128]{4,3,2,1,0:T(8,128)S(1)}, f32[4,8,5,8,128]{4,3,2,1,0:T(8,128)S(1)}) custom-call(f32[4,2,3,3,4,2,4,128]{7,6,5,4,3,2,1,0:T(4,128)S(1)} %get-tuple-element.24.u_ref, f32[4,8,4,8,128]{4,3,2,1,0:T(8,128)S(1)} %get-tuple-element.33.c_in, ...), custom_call_target="tpu_custom_call", output_to_operand_aliasing={{0}: (1, {}), {1}: (2, {})} | custom-call | flops 2000000 | bytes 6000000 | tf_op jit(solution)/shard_map/pallas_call | solution.py:503
  30.8 0.0 collective-permute-done.4.ft_ref
  30.9 2.7 %shard_map.42 = (f32[4,2,3,3,4,4,256]{6,5,4,3,2,1,0:T(4,128)}, f32[4,2,3,3,4,4,256]{6,5,4,3,2,1,0:T(4,128)}) custom-call(f32[4,2,3,3,4,2,4,128]{7,6,5,4,3,2,1,0:T(4,128)S(1)} %get-tuple-element.24.u_ref, f32[36,8,128]{2,1,0:T(8,128)S(1)} %collective-permute-done.low_ref, f32[48,8,128]{2,1,0:T(8,128)S(1)} %collective-permute-done.1.high_ref, ...), custom_call_target="tpu_custom_call" | custom-call | flops 3000000 | bytes 9000000 | tf_op jit(solution)/shard_map/pallas_call | solution.py:503
  33.5 0.0 collective-permute-done.8.row_ref
  33.5 0.7 %shard_map.44 = f32[2,3,3,1,4,256]{5,4,3,2,1,0:T(4,128)} custom-call(f32[2,3,3,8,128]{4,3,2,1,0:T(8,128)S(1)} %get-tuple-element.42.head_ref, f32[2,3,3,8,128]{4,3,2,1,0:T(8,128)S(1)} %collective-permute-done.8.row_ref, f32[2,3,3,8,128]{4,3,2,1,0:T(8,128)S(1)} %get-tuple-element.44.tail_ref), custom_call_target="tpu_custom_call" | custom-call | flops 1000000 | bytes 3000000 | tf_op jit(solution)/shard_map/pallas_call | solution.py:503
Async XLA Ops:
  2.0 17.0 %collective-permute-start.1 = (f32[48,8,128]{2,1,0:T(8,128)S(1)}, f32[48,8,128]{2,1,0:T(8,128)S(1)}, u32[]{:S(2)}, u32[]{:S(2)}) collective-permute-start(f32[48,8,128]{2,1,0:T(8,128)S(1)} %get-tuple-element.26), channel_id=1, source_target_pairs={{0,8},{8,16},{16,24},{24,32},{32,40},{40,48},{48,56},{56,64},{64,7... | collective-permute-start | bytes 589832 | tf_op jit(solution)/shard_map/ppermute | solution.py:517
  2.1 16.9 %collective-permute-start = (f32[36,8,128]{2,1,0:T(8,128)S(1)}, f32[36,8,128]{2,1,0:T(8,128)S(1)}, u32[]{:S(2)}, u32[]{:S(2)}) collective-permute-start(f32[36,8,128]{2,1,0:T(8,128)S(1)} %get-tuple-element.25), channel_id=1, source_target_pairs={{0,120},{8,0},{16,8},{24,16},{32,24},{40,32},{48,40},{56,48},{64,5... | collective-permute-start | bytes 442376 | tf_op jit(solution)/shard_map/ppermute | solution.py:517
  8.4 10.6 %collective-permute-start.2 = (f32[36,8,128]{2,1,0:T(8,128)S(1)}, f32[36,8,128]{2,1,0:T(8,128)S(1)}, u32[]{:S(2)}, u32[]{:S(2)}) collective-permute-start(f32[36,8,128]{2,1,0:T(8,128)S(1)} %get-tuple-element.27), channel_id=1, source_target_pairs={{0,7},{1,0},{2,1},{3,2},{4,3},{5,4},{6,5},{7,6},{8,15},{9,8},{10,9... | collective-permute-start | bytes 442376 | tf_op jit(solution)/shard_map/ppermute | solution.py:517
  11.4 7.6 %collective-permute-start.3 = (f32[24,128]{1,0:T(8,128)S(1)}, f32[24,128]{1,0:T(8,128)S(1)}, u32[]{:S(2)}, u32[]{:S(2)}) collective-permute-start(f32[24,128]{1,0:T(8,128)S(1)} %get-tuple-element.28), channel_id=1, source_target_pairs={{0,15},{1,8},{2,9},{3,10},{4,11},{5,12},{6,13},{7,14},{8,23},{9,16... | collective-permute-start | bytes 36872 | tf_op jit(solution)/shard_map/ppermute | solution.py:523
  20.1 7.2 %collective-permute-start.7 = (f32[2,3,3,8,128]{4,3,2,1,0:T(8,128)S(1)}, f32[2,3,3,8,128]{4,3,2,1,0:T(8,128)S(1)}, u32[]{:S(2)}, u32[]{:S(2)}) collective-permute-start(f32[2,3,3,8,128]{4,3,2,1,0:T(8,128)S(1)} %get-tuple-element.35.after_ref.s0_ref), channel_id=1, source_target_pairs={{0,1},{1,2},{2,3},{3,0},{4,5},{5,6},{6,7},{7,4},{8,9},{9,10},{10,1... | collective-permute-start | bytes 221192 | tf_op jit(solution)/shard_map/ppermute | solution.py:528
  20.2 7.1 %collective-permute-start.6 = (f32[2,3,3,8,128]{4,3,2,1,0:T(8,128)S(1)}, f32[2,3,3,8,128]{4,3,2,1,0:T(8,128)S(1)}, u32[]{:S(2)}, u32[]{:S(2)}) collective-permute-start(f32[2,3,3,8,128]{4,3,2,1,0:T(8,128)S(1)} %get-tuple-element.35.after_ref.s0_ref), channel_id=1, source_target_pairs={{0,2},{1,3},{2,0},{3,1},{4,6},{5,7},{6,4},{7,5},{8,10},{9,11},{10,... | collective-permute-start | bytes 221192 | tf_op jit(solution)/shard_map/ppermute | solution.py:528
  23.3 4.4 %collective-permute-start.5 = (f32[2,3,3,8,128]{4,3,2,1,0:T(8,128)S(1)}, f32[2,3,3,8,128]{4,3,2,1,0:T(8,128)S(1)}, u32[]{:S(2)}, u32[]{:S(2)}) collective-permute-start(f32[2,3,3,8,128]{4,3,2,1,0:T(8,128)S(1)} %get-tuple-element.35.after_ref.s0_ref), channel_id=1, source_target_pairs={{0,3},{1,0},{2,1},{3,2},{4,7},{5,4},{6,5},{7,6},{8,11},{9,8},{10,9... | collective-permute-start | bytes 221192 | tf_op jit(solution)/shard_map/ppermute | solution.py:528
  23.6 7.3 %collective-permute-start.4 = (f32[24,8,128]{2,1,0:T(8,128)S(1)}, f32[24,8,128]{2,1,0:T(8,128)S(1)}, u32[]{:S(2)}, u32[]{:S(2)}) collective-permute-start(f32[24,8,128]{2,1,0:T(8,128)S(1)} %get-tuple-element.32), channel_id=1, source_target_pairs={{0,1},{1,2},{2,3},{3,4},{4,5},{5,6},{6,7},{7,0},{8,9},{9,10},{10,1... | collective-permute-start | bytes 294920 | tf_op jit(solution)/shard_map/ppermute | solution.py:517
  27.8 5.7 %collective-permute-start.8 = (f32[2,3,3,8,128]{4,3,2,1,0:T(8,128)S(1)}, f32[2,3,3,8,128]{4,3,2,1,0:T(8,128)S(1)}, u32[]{:S(2)}, u32[]{:S(2)}) collective-permute-start(f32[2,3,3,8,128]{4,3,2,1,0:T(8,128)S(1)} %get-tuple-element.43), channel_id=1, source_target_pairs={{0,4},{1,5},{2,6},{3,7},{4,0},{5,1},{6,2},{7,3},{8,12},{9,13},{10,... | collective-permute-start | bytes 221192 | tf_op jit(solution)/shard_map/ppermute | solution.py:517

commit v3 on v2

--- a/solution.py
+++ b/solution.py
@@ -195,18 +195,13 @@
 LAST = pl.ds(3, 8, stride=4)
 
 
-def load_kernel(u_hbm, u_ref, st_ref, low_ref, high_ref, corner_ref, sem):
-    copies = {}
-    for d in range(4):
-        for h in range(2):
-            src = u_hbm.at[d, :, :, :, :, :, pl.ds(128 * h, 128)]
-            copies[d, h] = pltpu.make_async_copy(src, u_ref.at[d, :, :, :, :, h], sem.at[d, h])
-            copies[d, h].start()
+def load_kernel(u_hbm, u_ref, st_ref, lowt_ref, low_ref, high_ref, corner_ref, sem):
+    whole = pltpu.make_async_copy(u_hbm, u_ref, sem)
+    whole.start()
+    whole.wait()
     u = tiles(u_ref, (4, 2, 3, 3, 4))
     rows = u_ref.reshape(4, 2, 3, 3, 32, 128)
     for d in range(4):
-        for h in range(2):
-            copies[d, h].wait()
         for p in range(2):
             for i in range(2):
                 for j in range(3):
@@ -214,8 +209,10 @@
                     high_ref[d * 12 + k] = rows[d, p, i, j, LAST, :]
                     if d < 3:
                         st_ref[d * 12 + k] = u[d, p, i, j, 0]
-                    if d != 2:
-                        low_ref[min(d, 2) * 12 + k] = rows[d, p, i, j, FIRST, :]
+                    if d < 2:
+                        low_ref[d * 12 + k] = rows[d, p, i, j, FIRST, :]
+                    if d == 3:
+                        lowt_ref[k] = rows[d, p, i, j, FIRST, :]
                     if d == 2:
                         corner_ref[pl.ds(2 * k, 2), :] = rows[d, p, i, j, pl.ds(3, 2, stride=4), :]
 
@@ -277,9 +274,12 @@
     lax.fori_loop(0, 3, body, 0)
 
 
-def flat_kernel(u_ref, c_in, r_in, after_ref, c_ref, r_ref):
+def flat_kernel(u_ref, low_ref, high_ref, ab_ref, c_in, r_in, after_ref, c_ref, r_ref, x_ref):
     link = links(tiles(u_ref, (4, 2, 3, 3, 4)))
+    rows = u_ref.reshape(4, 2, 3, 3, 32, 128)
     m = masks()
+    line = lax.broadcasted_iota(jnp.int32, (8, 128), 0)
+    m["odd"] = (line & 1) == 1
 
     def body(t, carry):
         ux, uy, uz = link(0, t), link(1, t), link(2, t)
@@ -293,6 +293,22 @@
         return carry
 
     lax.fori_loop(0, 4, body, 0)
+    uz = packed(rows, 2, LAST)
+    uz_low = unpack_rows(high_ref, 2)
+    cz = [-ab_ref[8 + k] for k in range(8)]
+    rz = [jnp.where(line >= 2, pltpu.roll(ab_ref[k], 2, 0), 0.0) for k in range(8)]
+    for mu, shift in ((0, shift_x), (1, packed_shift_y)):
+        a, b = plane(packed(rows, mu, LAST), uz, unpack_rows(low_ref, mu), on_mat(uz, lambda v: shift(v, m, True)))
+        for k in range(8):
+            expand(x_ref, mu * 8 + k, -b[k], 3)
+        cz = [v + a[k] for k, v in enumerate(cz)]
+        rz = [v - shift(b[k], m, False) for k, v in enumerate(rz)]
+        a = corner_loop(unpack_rows(high_ref, mu), uz_low, packed(rows, mu, FIRST), on_mat(uz_low, lambda v: shift(v, m, True)), True)
+        for k in range(8):
+            expand(x_ref, 32 + mu * 8 + k, a[k], 0)
+    for k in range(8):
+        expand(x_ref, 16 + k, cz[k], 3)
+        expand(x_ref, 24 + k, rz[k], 3)
 
 
 def side_time(c_ref, r_ref, mu, shift, m, t, u_mu, u_t, mu_up):
@@ -348,19 +364,25 @@
     return put
 
 
-def time_kernel(u_ref, ht_ref, low_ref, high_ref, corner_ref, c_in, r_in, c_ref, r_ref, ft_ref, ab_ref, zt_ref, nt_ref, s_ref, x_ref, uz4_ref, pk_ref):
+def top_kernel(u_ref, ht_ref, c_in, r_in, c_ref, r_ref, uz4_ref):
+    link = links(tiles(u_ref, (4, 2, 3, 3, 4)))
+    m = masks()
+    put18(uz4_ref, unpack_rows(ht_ref, 2))
+    for mu, shift in ((0, shift_x), (1, shift_y)):
+        side_time(c_ref, r_ref, mu, shift, m, 3, link(mu, 3), link(3, 3), unpack_rows(ht_ref, mu))
+    zt_inside(c_ref, r_ref, m, 3, link(2, 3), link(3, 3), get18(uz4_ref))
+
+
+def time_kernel(u_ref, uz4_ref, lowt_ref, high_ref, corner_ref, c_ref, r_ref, ft_ref, ab_ref, zt_ref, nt_ref, s_ref, x_ref, pk_ref):
     link = links(tiles(u_ref, (4, 2, 3, 3, 4)))
     rows = u_ref.reshape(4, 2, 3, 3, 32, 128)
     zt, nt = tiles(zt_ref, (2, 3, 3, 4)), tiles(nt_ref, (2, 3, 3, 4))
-    m = masks()
-    above = unpack_rows(ht_ref, 2)
     for p in range(2):
         for i in range(3):
             for j in range(3):
-                uz4_ref[p, i, j] = above[i][j][p]
                 pk_ref[p, i, j, pl.ds(0, 6), :] = rows[2, p, i, j, pl.ds(11, 6, stride=4), :]
                 pk_ref[p, i, j, pl.ds(6, 2), :] = uz4_ref[p, i, j, pl.ds(3, 2, stride=4), :]
-    a, b = plane(packed(rows, 2, LAST), packed(rows, 3, LAST), get18(pk_ref), unpack_rows(low_ref, 2))
+    a, b = plane(packed(rows, 2, LAST), packed(rows, 3, LAST), get18(pk_ref), unpack_rows(lowt_ref, 0))
     for k in range(8):
         ab_ref[k] = a[k]
         ab_ref[8 + k] = b[k]
@@ -372,9 +394,6 @@
     b = corner_loop(unpack_rows(high_ref, 2), unpack_rows(high_ref, 3), up + [third_row(up)], packed(rows, 3, FIRST), False)
     for k in range(8):
         expand(x_ref, 8 + k, b[k], 0)
-    for mu, shift in ((0, shift_x), (1, shift_y)):
-        side_time(c_ref, r_ref, mu, shift, m, 3, link(mu, 3), link(3, 3), unpack_rows(ht_ref, mu))
-    zt_inside(c_ref, r_ref, m, 3, link(2, 3), link(3, 3), get18(uz4_ref))
     for mu in range(3):
         for k in range(8):
             v = r_ref[mu, k, 4]
@@ -395,37 +414,14 @@
 
 
 def out_copies(src, dst, sem, d):
-    return [pltpu.make_async_copy(src.at[:, :, :, :, h], dst.at[d, :, :, :, :, :, pl.ds(128 * h, 128)], sem.at[h]) for h in range(2)]
-
-
-def space_kernel(u_ref, low_ref, high_ref, ab_ref, ft_ref, c_ref, r_ref, zt_ref, nt_ref, new_hbm, z_hbm, zs_ref, ns_ref, x_ref, sem):
+    return [pltpu.make_async_copy(src.at[h], dst.at[d, h], sem.at[h]) for h in range(2)]
+
+
+def space_kernel(u_ref, x_ref, ft_ref, c_ref, r_ref, zt_ref, nt_ref, new_hbm, z_hbm, zs_ref, ns_ref, sem):
     link = links(tiles(u_ref, (4, 2, 3, 3, 4)))
-    rows = u_ref.reshape(4, 2, 3, 3, 32, 128)
     copies = out_copies(zt_ref, z_hbm, sem.at[6], 3) + out_copies(nt_ref, new_hbm, sem.at[7], 3)
     for c in copies:
         c.start()
-    m = masks()
-    line = lax.broadcasted_iota(jnp.int32, (8, 128), 0)
-    m["odd"] = (line & 1) == 1
-    uz = packed(rows, 2, LAST)
-    uz_low = unpack_rows(high_ref, 2)
-    cz = [-ab_ref[8 + k] for k in range(8)]
-    rz = [jnp.where(line >= 2, pltpu.roll(ab_ref[k], 2, 0), 0.0) for k in range(8)]
-    for mu, shift in ((0, shift_x), (1, packed_shift_y)):
-        a, b = plane(packed(rows, mu, LAST), uz, unpack_rows(low_ref, mu), on_mat(uz, lambda v: shift(v, m, True)))
-        for k in range(8):
-            expand(x_ref, mu * 8 + k, -b[k], 3)
-        cz = [v + a[k] for k, v in enumerate(cz)]
-        rz = [v - shift(b[k], m, False) for k, v in enumerate(rz)]
-        a = corner_loop(unpack_rows(high_ref, mu), uz_low, packed(rows, mu, FIRST), on_mat(uz_low, lambda v: shift(v, m, True)), True)
-        for k in range(8):
-            expand(x_ref, 32 + mu * 8 + k, a[k], 0)
-    for k in range(8):
-        expand(x_ref, 16 + k, cz[k], 3)
-        expand(x_ref, 24 + k, rz[k], 3)
-    for mu, first in ((0, 32), (1, 40), (2, 24)):
-        for k in range(8):
-            x_ref[first + k, at(0), :] += ft_ref[mu * 8 + k]
     for mu, first in ((0, 32), (1, 40), (2, 24)):
         zs, ns = tiles(zs_ref.at[mu], (2, 3, 3, 4)), tiles(ns_ref.at[mu], (2, 3, 3, 4))
 
@@ -433,6 +429,8 @@
             u = link(mu, t)
             w = transport(u, [c_ref[mu, k, t] + x_ref[mu * 8 + k, at(t), :] for k in range(8)])
             f = [w[k] + (r_ref[mu, k, t] + x_ref[first + k, at(t), :]) for k in range(8)]
+            below = jnp.where(t == 0, 1.0, 0.0)
+            f = [v + below * ft_ref[mu * 8 + k] for k, v in enumerate(f)]
             finish(f, u, writer(zs, t=t), writer(ns, t=t))
             return carry
 
@@ -487,7 +485,7 @@
     put18(tiles(o_ref, (2, 3, 3)), loop)
     copies = []
     for h in range(2):
-        copies.append(pltpu.make_async_copy(o_ref.at[:, :, :, h], out_hbm.at[:, :, :, 0, :, pl.ds(128 * h, 128)], sem.at[h]))
+        copies.append(pltpu.make_async_copy(o_ref.at[h], out_hbm.at[h], sem.at[h]))
     for c in copies:
         c.start()
     for c in copies:
@@ -528,54 +526,64 @@
     return lax.ppermute(x, "tm", [(i, i // ROW * ROW + (i - k) % ROW) for i in range(n)])
 
 
+def plain(x, slices):
+    return jnp.swapaxes(x, -3, -2).reshape(*x.shape[: -4 if slices > 1 else -3], slices, 4, 256)
+
+
 def program(gauge_links):
     dma = pltpu.SemaphoreType.DMA
     whole = (4, 2, 3, 3, 4, 2, 4, 128)
     mat18 = ("v", (2, 3, 3, 8, 128))
-    full = ("h", gauge_links.shape)
+    full = ("h", whole)
+    gauge_links = jnp.swapaxes(gauge_links.reshape(4, 2, 3, 3, 4, 4, 2, 128), 5, 6)
 
     def pack(n):
         return ("v", (n, 8, 128))
 
-    u, st, low, high, corner = call(
-        load_kernel, [("v", whole), pack(36), pack(36), pack(48), ("v", (24, 128))], [("h", gauge_links)], [dma((4, 2))]
+    u, st, lowt, low, high, corner = call(
+        load_kernel,
+        [("v", whole), pack(36), pack(12), pack(24), pack(48), ("v", (24, 128))],
+        [("h", gauge_links)],
+        [dma(())],
     )
     u = ("v", u)
     high = ("v", from_ahead(high, "space", -1))
     corner = ("v", diagonal(corner))
     ht = ("v", from_ahead(st, "tm", 1))
+    lowt = ("v", from_ahead(lowt, "space", 1))
     low = ("v", from_ahead(low, "space", 1))
     acc = [("v", (4, 8, 4, 8, 128)), ("v", (4, 8, 5, 8, 128))]
     slices = ("v", (2, 3, 3, 4, 2, 4, 128))
     c, r = call(steep_kernel, acc, [u], us=1.5)
-    c, r, ft, ab, zt, nt, s = call(
+    c, r, uz4 = call(top_kernel, [*acc, mat18], [u, ht, ("v", c), ("v", r)], (), {2: 0, 3: 1}, us=0.5)
+    ft, ab, zt, nt, s = call(
         time_kernel,
-        [*acc, pack(24), pack(16), slices, slices, mat18],
-        [u, ht, low, high, corner, ("v", c), ("v", r)],
-        [VMEM((16, 32, 128), F32), VMEM((2, 3, 3, 8, 128), F32), VMEM((2, 3, 3, 8, 128), F32)],
-        {5: 0, 6: 1},
-        us=1.4,
+        [pack(24), pack(16), slices, slices, mat18],
+        [u, ("v", uz4), lowt, high, corner, ("v", c), ("v", r)],
+        [VMEM((16, 32, 128), F32), VMEM((2, 3, 3, 8, 128), F32)],
+        us=0.7,
     )
     s1, s3, s2 = in_row(s, 1), in_row(s, 3), in_row(s, 2)
     ft = ("v", from_ahead(ft, "tm", -1))
-    c, r = call(flat_kernel, acc, [u, ("v", c), ("v", r), ("v", s)], (), {1: 0, 2: 1}, us=2.0)
+    edges = ("v", (48, 32, 128))
+    c, r, x = call(flat_kernel, [*acc, edges], [u, low, high, ("v", ab), ("v", c), ("v", r), ("v", s)], (), {4: 0, 5: 1}, us=2.6)
     head, tail, row = call(join_kernel, [mat18] * 3, [("v", s), ("v", s1), ("v", s2), ("v", s3)], us=0.1)
     row = from_ahead(row, "tm", ROW)
     stage = VMEM((3, 2, 3, 3, 4, 2, 4, 128), F32)
     new, force = call(
         space_kernel,
         [full, full],
-        [u, low, high, ("v", ab), ft, ("v", c), ("v", r), ("v", zt), ("v", nt)],
-        [stage, stage, VMEM((48, 32, 128), F32), dma((8, 2))],
+        [u, ("v", x), ft, ("v", c), ("v", r), ("v", zt), ("v", nt)],
+        [stage, stage, dma((8, 2))],
         us=3.0,
     )
     (hol,) = call(
         holonomy_kernel,
-        [("h", (2, 3, 3, 1, *gauge_links.shape[5:]))],
+        [("h", (2, 3, 3, 2, 4, 128))],
         [("v", head), ("v", row), ("v", tail)],
         [VMEM((2, 3, 3, 2, 4, 128), F32), dma((2,))],
     )
-    return new, force, hol
+    return plain(new, 4), plain(force, 4), plain(hol, 1)
 
 
 def solution(mesh):

time: 34.4 us -> 34.2 us (level); the launches traced: 34.2 us -> 33.5 us
  starting transfers between devices: 15.6 us -> 14.3 us
  waiting for transfers between devices: 8.77 us -> 9.46 us
    ppermute x5 -> x6, starting transfers between devices: 12.2 us -> 11 us  [from_ahead(): return lax.ppermute(x, axis, [(i, (i - k) % n) for i in range(n)])]
    ppermute x5 -> x6, waiting for transfers between devices: 0.01 us -> 0.65 us  [from_ahead(): return lax.ppermute(x, axis, [(i, (i - k) % n) for i in range(n)])]
    ppermute x3, waiting for transfers between devices: 2.33 us -> 2.76 us  [in_row(): lax.ppermute(x, 'tm', [(i, i // ROW * ROW + (i - k) % ROW) for i in range...]
    ppermute x1, waiting for transfers between devices: 6.43 us -> 6.05 us  [diagonal(): return lax.ppermute(x, ('space', 'tm'), pairs)]
    pallas_call x7 -> x8, Pallas kernels: 9.14 us -> 9.04 us  [call(): pl.pallas_call(kernel, out_shape=shapes, in_specs=[spec(k) for k, _ in ar...]
  transfers between devices with their start and end apart: 9 -> 10, of which waited for: 3 -> 4; matrix products, arithmetic and copies ran while one was open for 0% -> 0% of each run, Pallas kernels for 17% -> 19%
where the time goes in v3:
time: 34.2 us; the launch traced here: 33.5 us
  starting transfers between devices  14.3 us (42%)
  waiting for transfers between devices  9.46 us (28%)
  Pallas kernels  9.04 us (26%)
  between operations  0.72 us (2%)
    ppermute x6, starting transfers between devices, from_ahead(): return lax.ppermute(x, axis, [(i, (i - k) % n) for i in range(n)])  11 us
    pallas_call x8, Pallas kernels, call(): pl.pallas_call(kernel, out_shape=shapes, in_specs=[spec(k) for k, _ in ar...  9.04 us
    ppermute x1, waiting for transfers between devices, diagonal(): return lax.ppermute(x, ('space', 'tm'), pairs)  6.05 us
    ppermute x3, starting transfers between devices, in_row(): lax.ppermute(x, 'tm', [(i, i // ROW * ROW + (i - k) % ROW) for i in range...  3.3 us
    ppermute x3, waiting for transfers between devices, in_row(): lax.ppermute(x, 'tm', [(i, i // ROW * ROW + (i - k) % ROW) for i in range...  2.76 us
  transfers between devices with their start and end apart: 10, of which 4 were waited for; matrix products, arithmetic and copies ran while one was open for 0% of the time, Pallas kernels for 19%

profile of v3, /device:TPU:0, one launch (start us, length us, event | category | flops | bytes accessed | tf_op | source)
XLA Modules:
  0.0 33.5 jit_solution(12397018936250141136)
XLA Ops:
  0.6 1.3 %shard_map.38 = (f32[4,2,3,3,4,2,4,128]{7,6,5,4,3,2,1,0:T(4,128)S(1)}, f32[36,8,128]{2,1,0:T(8,128)S(1)}, f32[12,8,128]{2,1,0:T(8,128)S(1)}, f32[24,8,128]{2,1,0...) custom-call(f32[4,2,3,3,4,2,4,128]{7,6,5,4,3,2,1,0:T(4,128)} %bitcast.12), custom_call_target="tpu_custom_call" | custom-call | flops 1000000 | bytes 3000000 | tf_op jit(solution)/shard_map/pallas_call | solution.py:501
  2.0 0.1 collective-permute-start.1
  2.1 4.0 %collective-permute-start.2 = (f32[36,8,128]{2,1,0:T(8,128)S(1)}, f32[36,8,128]{2,1,0:T(8,128)S(1)}, u32[]{:S(2)}, u32[]{:S(2)}) collective-permute-start(f32[36,8,128]{2,1,0:T(8,128)S(1)} %get-tuple-element.30), channel_id=1, source_target_pairs={{0,7},{1,0},{2,1},{3,2},{4,3},{5,4},{6,5},{7,6},{8,15},{9,8},{10,9... | collective-permute-start | bytes 442376 | tf_op jit(solution)/shard_map/ppermute | solution.py:515
  6.0 5.6 %collective-permute-start.3 = (f32[12,8,128]{2,1,0:T(8,128)S(1)}, f32[12,8,128]{2,1,0:T(8,128)S(1)}, u32[]{:S(2)}, u32[]{:S(2)}) collective-permute-start(f32[12,8,128]{2,1,0:T(8,128)S(1)} %get-tuple-element.34), channel_id=1, source_target_pairs={{0,120},{8,0},{16,8},{24,16},{32,24},{40,32},{48,40},{56,48},{64,5... | collective-permute-start | bytes 147464 | tf_op jit(solution)/shard_map/ppermute | solution.py:515
  11.6 0.0 collective-permute-start.4
  11.6 1.2 %shard_map.39 = (f32[4,8,4,8,128]{4,3,2,1,0:T(8,128)S(1)}, f32[4,8,5,8,128]{4,3,2,1,0:T(8,128)S(1)}) custom-call(f32[4,2,3,3,4,2,4,128]{7,6,5,4,3,2,1,0:T(4,128)S(1)} %get-tuple-element.27.u_ref), custom_call_target="tpu_custom_call" | custom-call | flops 1500000 | bytes 4500000 | tf_op jit(solution)/shard_map/pallas_call | solution.py:501
  12.8 0.0 collective-permute-done.2.ht_ref
  12.8 0.4 %shard_map.40 = (f32[4,8,4,8,128]{4,3,2,1,0:T(8,128)S(1)}, f32[4,8,5,8,128]{4,3,2,1,0:T(8,128)S(1)}, f32[2,3,3,8,128]{4,3,2,1,0:T(8,128)S(1)}) custom-call(f32[4,2,3,3,4,2,4,128]{7,6,5,4,3,2,1,0:T(4,128)S(1)} %get-tuple-element.27.u_ref, f32[36,8,128]{2,1,0:T(8,128)S(1)} %collective-permute-done.2.ht_ref, ...), custom_call_target="tpu_custom_call", output_to_operand_aliasing={{0}: (2, {}), {1}: (3, {})} | custom-call | flops 500000 | bytes 1500000 | tf_op jit(solution)/shard_map/pallas_call | solution.py:501
  13.2 6.0 %collective-permute-done.4.corner_ref = f32[24,128]{1,0:T(8,128)S(1)} collective-permute-done((f32[24,128]{1,0:T(8,128)S(1)}, f32[24,128]{1,0:T(8,128)S(1)}, u32[]{:S(2)}, u32[]{:S(2)}) %collective-permute-start.4) | collective-permute-done | bytes 12320 | tf_op jit(solution)/shard_map/ppermute | solution.py:521
  19.2 0.0 collective-permute-done.3.lowt_ref
  19.2 0.0 collective-permute-done.1.high_ref
  19.2 0.7 %shard_map.41 = (f32[24,8,128]{2,1,0:T(8,128)S(1)}, f32[16,8,128]{2,1,0:T(8,128)S(1)}, f32[2,3,3,4,2,4,128]{6,5,4,3,2,1,0:T(4,128)S(1)}, f32[2,3,3,4,2,4,128]{6,...) custom-call(f32[4,2,3,3,4,2,4,128]{7,6,5,4,3,2,1,0:T(4,128)S(1)} %get-tuple-element.27.u_ref, ...), custom_call_target="tpu_custom_call" | custom-call | flops 700000 | bytes 2100000 | tf_op jit(solution)/shard_map/pallas_call | solution.py:501
  20.0 0.1 collective-permute-start.8
  20.1 2.4 %collective-permute-start.7 = (f32[2,3,3,8,128]{4,3,2,1,0:T(8,128)S(1)}, f32[2,3,3,8,128]{4,3,2,1,0:T(8,128)S(1)}, u32[]{:S(2)}, u32[]{:S(2)}) collective-permute-start(f32[2,3,3,8,128]{4,3,2,1,0:T(8,128)S(1)} %get-tuple-element.39.after_ref.s0_ref), channel_id=1, source_target_pairs={{0,2},{1,3},{2,0},{3,1},{4,6},{5,7},{6,4},{7,5},{8,10},{9,11},{10,... | collective-permute-start | bytes 221192 | tf_op jit(solution)/shard_map/ppermute | solution.py:526
  22.5 0.8 %collective-permute-start.6 = (f32[2,3,3,8,128]{4,3,2,1,0:T(8,128)S(1)}, f32[2,3,3,8,128]{4,3,2,1,0:T(8,128)S(1)}, u32[]{:S(2)}, u32[]{:S(2)}) collective-permute-start(f32[2,3,3,8,128]{4,3,2,1,0:T(8,128)S(1)} %get-tuple-element.39.after_ref.s0_ref), channel_id=1, source_target_pairs={{0,3},{1,0},{2,1},{3,2},{4,7},{5,4},{6,5},{7,6},{8,11},{9,8},{10,9... | collective-permute-start | bytes 221192 | tf_op jit(solution)/shard_map/ppermute | solution.py:526
  23.3 0.0 collective-permute-start
  23.3 1.2 %collective-permute-start.5 = (f32[24,8,128]{2,1,0:T(8,128)S(1)}, f32[24,8,128]{2,1,0:T(8,128)S(1)}, u32[]{:S(2)}, u32[]{:S(2)}) collective-permute-start(f32[24,8,128]{2,1,0:T(8,128)S(1)} %get-tuple-element.41), channel_id=1, source_target_pairs={{0,1},{1,2},{2,3},{3,4},{4,5},{5,6},{6,7},{7,0},{8,9},{9,10},{10,1... | collective-permute-start | bytes 294920 | tf_op jit(solution)/shard_map/ppermute | solution.py:515
  24.5 1.9 %collective-permute-done.8.s3_ref = f32[2,3,3,8,128]{4,3,2,1,0:T(8,128)S(1)} collective-permute-done((f32[2,3,3,8,128]{4,3,2,1,0:T(8,128)S(1)}, f32[2,3,3,8,128]{4,3,2,1,0:T(8,128)S(1)}, u32[]{:S(2)}, u32[]{:S(2)}) %collective-permute-start.8) | collective-permute-done | bytes 73760 | tf_op jit(solution)/shard_map/ppermute | solution.py:526
  26.4 0.0 collective-permute-done.7.s2_ref
  26.4 0.9 %collective-permute-done.6.s1_ref = f32[2,3,3,8,128]{4,3,2,1,0:T(8,128)S(1)} collective-permute-done((f32[2,3,3,8,128]{4,3,2,1,0:T(8,128)S(1)}, f32[2,3,3,8,128]{4,3,2,1,0:T(8,128)S(1)}, u32[]{:S(2)}, u32[]{:S(2)}) %collective-permute-start.6) | collective-permute-done | bytes 73760 | tf_op jit(solution)/shard_map/ppermute | solution.py:526
  27.3 0.1 shard_map.44
  27.4 0.1 collective-permute-start.9
  27.5 0.0 collective-permute-done.low_ref
  27.5 2.4 %shard_map.42 = (f32[4,8,4,8,128]{4,3,2,1,0:T(8,128)S(1)}, f32[4,8,5,8,128]{4,3,2,1,0:T(8,128)S(1)}, f32[48,32,128]{2,1,0:T(8,128)S(1)}) custom-call(f32[4,2,3,3,4,2,4,128]{7,6,5,4,3,2,1,0:T(4,128)S(1)} %get-tuple-element.27.u_ref, f32[24,8,128]{2,1,0:T(8,128)S(1)} %collective-permute-done.low_ref, ...), custom_call_target="tpu_custom_call", output_to_operand_aliasing={{0}: (4, {}), {1}: (5, {})} | custom-call | flops 2600000 | bytes 7800000 | tf_op jit(solution)/shard_map/pallas_call | solution.py:501
  30.0 0.6 %collective-permute-done.5.ft_ref = f32[24,8,128]{2,1,0:T(8,128)S(1)} collective-permute-done((f32[24,8,128]{2,1,0:T(8,128)S(1)}, f32[24,8,128]{2,1,0:T(8,128)S(1)}, u32[]{:S(2)}, u32[]{:S(2)}) %collective-permute-start.5) | collective-permute-done | bytes 98336 | tf_op jit(solution)/shard_map/ppermute | solution.py:515
  30.6 2.2 %shard_map.43 = (f32[4,2,3,3,4,2,4,128]{7,6,5,4,3,2,1,0:T(4,128)}, f32[4,2,3,3,4,2,4,128]{7,6,5,4,3,2,1,0:T(4,128)}) custom-call(f32[4,2,3,3,4,2,4,128]{7,6,5,4,3,2,1,0:T(4,128)S(1)} %get-tuple-element.27.u_ref, f32[48,32,128]{2,1,0:T(8,128)S(1)} %get-tuple-element.40.x_ref, f32[24,8,128]{2,1,0:T(8,128)S(1)} %collective-permute-done.5.ft_ref, ...), custom_call_target="tpu_custom_call" | custom-call | flops 3000000 | bytes 9000000 | tf_op jit(solution)/shard_map/pallas_call | solution.py:501
  32.8 0.0 collective-permute-done.9.row_ref
  32.8 0.7 %shard_map.45 = f32[2,3,3,2,4,128]{5,4,3,2,1,0:T(4,128)} custom-call(f32[2,3,3,8,128]{4,3,2,1,0:T(8,128)S(1)} %get-tuple-element.48.head_ref, f32[2,3,3,8,128]{4,3,2,1,0:T(8,128)S(1)} %collective-permute-done.9.row_ref, f32[2,3,3,8,128]{4,3,2,1,0:T(8,128)S(1)} %get-tuple-element.50.tail_ref), custom_call_target="tpu_custom_call" | custom-call | flops 1000000 | bytes 3000000 | tf_op jit(solution)/shard_map/pallas_call | solution.py:501
Async XLA Ops:
  2.0 17.3 %collective-permute-start.1 = (f32[48,8,128]{2,1,0:T(8,128)S(1)}, f32[48,8,128]{2,1,0:T(8,128)S(1)}, u32[]{:S(2)}, u32[]{:S(2)}) collective-permute-start(f32[48,8,128]{2,1,0:T(8,128)S(1)} %get-tuple-element.29), channel_id=1, source_target_pairs={{0,8},{8,16},{16,24},{24,32},{32,40},{40,48},{48,56},{56,64},{64,7... | collective-permute-start | bytes 589832 | tf_op jit(solution)/shard_map/ppermute | solution.py:515
  2.1 10.8 %collective-permute-start.2 = (f32[36,8,128]{2,1,0:T(8,128)S(1)}, f32[36,8,128]{2,1,0:T(8,128)S(1)}, u32[]{:S(2)}, u32[]{:S(2)}) collective-permute-start(f32[36,8,128]{2,1,0:T(8,128)S(1)} %get-tuple-element.30), channel_id=1, source_target_pairs={{0,7},{1,0},{2,1},{3,2},{4,3},{5,4},{6,5},{7,6},{8,15},{9,8},{10,9... | collective-permute-start | bytes 442376 | tf_op jit(solution)/shard_map/ppermute | solution.py:515
  6.0 13.2 %collective-permute-start.3 = (f32[12,8,128]{2,1,0:T(8,128)S(1)}, f32[12,8,128]{2,1,0:T(8,128)S(1)}, u32[]{:S(2)}, u32[]{:S(2)}) collective-permute-start(f32[12,8,128]{2,1,0:T(8,128)S(1)} %get-tuple-element.34), channel_id=1, source_target_pairs={{0,120},{8,0},{16,8},{24,16},{32,24},{40,32},{48,40},{56,48},{64,5... | collective-permute-start | bytes 147464 | tf_op jit(solution)/shard_map/ppermute | solution.py:515
  11.6 7.6 %collective-permute-start.4 = (f32[24,128]{1,0:T(8,128)S(1)}, f32[24,128]{1,0:T(8,128)S(1)}, u32[]{:S(2)}, u32[]{:S(2)}) collective-permute-start(f32[24,128]{1,0:T(8,128)S(1)} %get-tuple-element.35), channel_id=1, source_target_pairs={{0,15},{1,8},{2,9},{3,10},{4,11},{5,12},{6,13},{7,14},{8,23},{9,16... | collective-permute-start | bytes 36872 | tf_op jit(solution)/shard_map/ppermute | solution.py:521
  20.0 6.4 %collective-permute-start.8 = (f32[2,3,3,8,128]{4,3,2,1,0:T(8,128)S(1)}, f32[2,3,3,8,128]{4,3,2,1,0:T(8,128)S(1)}, u32[]{:S(2)}, u32[]{:S(2)}) collective-permute-start(f32[2,3,3,8,128]{4,3,2,1,0:T(8,128)S(1)} %get-tuple-element.39.after_ref.s0_ref), channel_id=1, source_target_pairs={{0,1},{1,2},{2,3},{3,0},{4,5},{5,6},{6,7},{7,4},{8,9},{9,10},{10,1... | collective-permute-start | bytes 221192 | tf_op jit(solution)/shard_map/ppermute | solution.py:526
  20.1 6.3 %collective-permute-start.7 = (f32[2,3,3,8,128]{4,3,2,1,0:T(8,128)S(1)}, f32[2,3,3,8,128]{4,3,2,1,0:T(8,128)S(1)}, u32[]{:S(2)}, u32[]{:S(2)}) collective-permute-start(f32[2,3,3,8,128]{4,3,2,1,0:T(8,128)S(1)} %get-tuple-element.39.after_ref.s0_ref), channel_id=1, source_target_pairs={{0,2},{1,3},{2,0},{3,1},{4,6},{5,7},{6,4},{7,5},{8,10},{9,11},{10,... | collective-permute-start | bytes 221192 | tf_op jit(solution)/shard_map/ppermute | solution.py:526
  22.5 4.8 %collective-permute-start.6 = (f32[2,3,3,8,128]{4,3,2,1,0:T(8,128)S(1)}, f32[2,3,3,8,128]{4,3,2,1,0:T(8,128)S(1)}, u32[]{:S(2)}, u32[]{:S(2)}) collective-permute-start(f32[2,3,3,8,128]{4,3,2,1,0:T(8,128)S(1)} %get-tuple-element.39.after_ref.s0_ref), channel_id=1, source_target_pairs={{0,3},{1,0},{2,1},{3,2},{4,7},{5,4},{6,5},{7,6},{8,11},{9,8},{10,9... | collective-permute-start | bytes 221192 | tf_op jit(solution)/shard_map/ppermute | solution.py:526
  23.3 4.2 %collective-permute-start = (f32[24,8,128]{2,1,0:T(8,128)S(1)}, f32[24,8,128]{2,1,0:T(8,128)S(1)}, u32[]{:S(2)}, u32[]{:S(2)}) collective-permute-start(f32[24,8,128]{2,1,0:T(8,128)S(1)} %get-tuple-element.28), channel_id=1, source_target_pairs={{0,120},{8,0},{16,8},{24,16},{32,24},{40,32},{48,40},{56,48},{64,5... | collective-permute-start | bytes 294920 | tf_op jit(solution)/shard_map/ppermute | solution.py:515
  23.3 7.3 %collective-permute-start.5 = (f32[24,8,128]{2,1,0:T(8,128)S(1)}, f32[24,8,128]{2,1,0:T(8,128)S(1)}, u32[]{:S(2)}, u32[]{:S(2)}) collective-permute-start(f32[24,8,128]{2,1,0:T(8,128)S(1)} %get-tuple-element.41), channel_id=1, source_target_pairs={{0,1},{1,2},{2,3},{3,4},{4,5},{5,6},{6,7},{7,0},{8,9},{9,10},{10,1... | collective-permute-start | bytes 294920 | tf_op jit(solution)/shard_map/ppermute | solution.py:515
  27.4 5.4 %collective-permute-start.9 = (f32[2,3,3,8,128]{4,3,2,1,0:T(8,128)S(1)}, f32[2,3,3,8,128]{4,3,2,1,0:T(8,128)S(1)}, u32[]{:S(2)}, u32[]{:S(2)}) collective-permute-start(f32[2,3,3,8,128]{4,3,2,1,0:T(8,128)S(1)} %get-tuple-element.49), channel_id=1, source_target_pairs={{0,4},{1,5},{2,6},{3,7},{4,0},{5,1},{6,2},{7,3},{8,12},{9,13},{10,... | collective-permute-start | bytes 221192 | tf_op jit(solution)/shard_map/ppermute | solution.py:515

commit v4 on v3

--- a/solution.py
+++ b/solution.py
@@ -160,15 +160,20 @@
     return [[(f(a), f(b)) for a, b in row] for row in m]
 
 
+def special(a, b, ha=False, hb=False):
+    m = [[entry(terms(a, ha, b, hb, i, j)) for j in range(3)] for i in range(2)]
+    return m + [third_row(m)]
+
+
 def plane(u_mu, u_nu, mu_up, nu_up):
-    d = product(u_mu, u_nu, ha=True)
-    g = product(mu_up, nu_up, hb=True)
+    d = special(u_mu, u_nu, ha=True)
+    g = special(mu_up, nu_up, hb=True)
     return twice_ta(g, d), twice_ta(d, g)
 
 
 def corner_loop(u_mu, u_nu, mu_up, nu_up, at_nu):
-    d = product(u_mu, u_nu, ha=True)
-    g = product(mu_up, nu_up, hb=True)
+    d = special(u_mu, u_nu, ha=True)
+    g = special(mu_up, nu_up, hb=True)
     return twice_ta(g, d) if at_nu else twice_ta(d, g)
 
 
@@ -196,9 +201,10 @@
 
 
 def load_kernel(u_hbm, u_ref, st_ref, lowt_ref, low_ref, high_ref, corner_ref, sem):
-    whole = pltpu.make_async_copy(u_hbm, u_ref, sem)
-    whole.start()
-    whole.wait()
+    two = pl.ds(0, 2)
+    copy = pltpu.make_async_copy(u_hbm.at[:, :, two], u_ref.at[:, :, two], sem)
+    copy.start()
+    copy.wait()
     u = tiles(u_ref, (4, 2, 3, 3, 4))
     rows = u_ref.reshape(4, 2, 3, 3, 32, 128)
     for d in range(4):
@@ -241,15 +247,6 @@
     return lambda d, t: mat(lambda p, i, j: u[d, p, i, j, t])
 
 
-def side_z(c_ref, r_ref, mu, shift, m, t, u_mu, u_z):
-    a, b = plane(u_mu, u_z, on_mat(u_mu, next_z), on_mat(u_z, lambda v: shift(v, m, True)))
-    b = inside(b, m)
-    accumulate(c_ref, 2, t, inside(a, m))
-    accumulate(c_ref, mu, t, b, -1)
-    accumulate(r_ref, mu, t, [down_z(v, m) for v in a])
-    accumulate(r_ref, 2, t, [shift(v, m, False) for v in b], -1)
-
-
 def zt_inside(c_ref, r_ref, m, t, u_z, u_t, z_up):
     a, b = plane(u_z, u_t, z_up, on_mat(u_t, next_z))
     a = inside(a, m)
@@ -259,8 +256,19 @@
     accumulate(r_ref, 3, t, [down_z(v, m) for v in b], -1)
 
 
-def steep_kernel(u_ref, c_ref, r_ref):
-    link = links(tiles(u_ref, (4, 2, 3, 3, 4)))
+def steep_kernel(u_in, u_ref, c_ref, r_ref):
+    u = tiles(u_ref, (4, 2, 3, 3, 4))
+
+    def complete(t, carry):
+        for d in range(4):
+            row = third_row([[(u[d, 0, i, j, t], u[d, 1, i, j, t]) for j in range(3)] for i in range(2)])
+            for j in range(3):
+                for p in range(2):
+                    u[d, p, 2, j, t] = row[j][p]
+        return carry
+
+    lax.fori_loop(0, 4, complete, 0)
+    link = links(u)
     m = masks()
     c_ref[...] = jnp.zeros_like(c_ref)
     r_ref[...] = jnp.zeros_like(r_ref)
@@ -274,41 +282,44 @@
     lax.fori_loop(0, 3, body, 0)
 
 
-def flat_kernel(u_ref, low_ref, high_ref, ab_ref, c_in, r_in, after_ref, c_ref, r_ref, x_ref):
+def flat_kernel(u_ref, low_ref, high_ref, ab_ref, c_in, r_in, after_ref, c_ref, r_ref, x_ref, above_ref):
     link = links(tiles(u_ref, (4, 2, 3, 3, 4)))
     rows = u_ref.reshape(4, 2, 3, 3, 32, 128)
     m = masks()
     line = lax.broadcasted_iota(jnp.int32, (8, 128), 0)
     m["odd"] = (line & 1) == 1
+    for mu in range(2):
+        halo = unpack_rows(low_ref, mu)
+        for i in range(3):
+            for j in range(3):
+                for p in range(2):
+                    above_ref[mu, p, i, j, LAST, :] = halo[i][j][p]
 
     def body(t, carry):
-        ux, uy, uz = link(0, t), link(1, t), link(2, t)
-        a, b = plane(ux, uy, on_mat(ux, lambda v: shift_y(v, m, True)), on_mat(uy, lambda v: shift_x(v, m, True)))
+        us = [link(d, t) for d in range(3)]
+        a, b = plane(us[0], us[1], on_mat(us[0], lambda v: shift_y(v, m, True)), on_mat(us[1], lambda v: shift_x(v, m, True)))
         accumulate(c_ref, 1, t, a)
         accumulate(c_ref, 0, t, b, -1)
         accumulate(r_ref, 0, t, [shift_y(v, m, False) for v in a])
         accumulate(r_ref, 1, t, [shift_x(v, m, False) for v in b], -1)
-        side_z(c_ref, r_ref, 0, shift_x, m, t, ux, uz)
-        side_z(c_ref, r_ref, 1, shift_y, m, t, uy, uz)
+        for mu, shift in ((0, shift_x), (1, shift_y)):
+            up = mat(lambda p, i, j: jnp.where(m["z"] == 3, above_ref[mu, p, i, j, at(t), :], next_z(us[mu][i][j][p])))
+            a, b = plane(us[mu], us[2], up, on_mat(us[2], lambda v: shift(v, m, True)))
+            accumulate(c_ref, 2, t, a)
+            accumulate(c_ref, mu, t, b, -1)
+            accumulate(r_ref, mu, t, [down_z(v, m) for v in a])
+            accumulate(r_ref, 2, t, [shift(v, m, False) for v in b], -1)
         return carry
 
     lax.fori_loop(0, 4, body, 0)
-    uz = packed(rows, 2, LAST)
     uz_low = unpack_rows(high_ref, 2)
-    cz = [-ab_ref[8 + k] for k in range(8)]
-    rz = [jnp.where(line >= 2, pltpu.roll(ab_ref[k], 2, 0), 0.0) for k in range(8)]
     for mu, shift in ((0, shift_x), (1, packed_shift_y)):
-        a, b = plane(packed(rows, mu, LAST), uz, unpack_rows(low_ref, mu), on_mat(uz, lambda v: shift(v, m, True)))
-        for k in range(8):
-            expand(x_ref, mu * 8 + k, -b[k], 3)
-        cz = [v + a[k] for k, v in enumerate(cz)]
-        rz = [v - shift(b[k], m, False) for k, v in enumerate(rz)]
         a = corner_loop(unpack_rows(high_ref, mu), uz_low, packed(rows, mu, FIRST), on_mat(uz_low, lambda v: shift(v, m, True)), True)
         for k in range(8):
-            expand(x_ref, 32 + mu * 8 + k, a[k], 0)
+            expand(x_ref, 16 + mu * 8 + k, a[k], 0)
     for k in range(8):
-        expand(x_ref, 16 + k, cz[k], 3)
-        expand(x_ref, 24 + k, rz[k], 3)
+        expand(x_ref, k, -ab_ref[8 + k], 3)
+        expand(x_ref, 8 + k, jnp.where(line >= 2, pltpu.roll(ab_ref[k], 2, 0), 0.0), 3)
 
 
 def side_time(c_ref, r_ref, mu, shift, m, t, u_mu, u_t, mu_up):
@@ -422,12 +433,15 @@
     copies = out_copies(zt_ref, z_hbm, sem.at[6], 3) + out_copies(nt_ref, new_hbm, sem.at[7], 3)
     for c in copies:
         c.start()
-    for mu, first in ((0, 32), (1, 40), (2, 24)):
+    for mu, first in ((0, 16), (1, 24), (2, 8)):
         zs, ns = tiles(zs_ref.at[mu], (2, 3, 3, 4)), tiles(ns_ref.at[mu], (2, 3, 3, 4))
 
         def body(t, carry):
             u = link(mu, t)
-            w = transport(u, [c_ref[mu, k, t] + x_ref[mu * 8 + k, at(t), :] for k in range(8)])
+            c = [c_ref[mu, k, t] for k in range(8)]
+            if mu == 2:
+                c = [v + x_ref[k, at(t), :] for k, v in enumerate(c)]
+            w = transport(u, c)
             f = [w[k] + (r_ref[mu, k, t] + x_ref[first + k, at(t), :]) for k in range(8)]
             below = jnp.where(t == 0, 1.0, 0.0)
             f = [v + below * ft_ref[mu * 8 + k] for k, v in enumerate(f)]
@@ -546,7 +560,6 @@
         [("h", gauge_links)],
         [dma(())],
     )
-    u = ("v", u)
     high = ("v", from_ahead(high, "space", -1))
     corner = ("v", diagonal(corner))
     ht = ("v", from_ahead(st, "tm", 1))
@@ -554,7 +567,8 @@
     low = ("v", from_ahead(low, "space", 1))
     acc = [("v", (4, 8, 4, 8, 128)), ("v", (4, 8, 5, 8, 128))]
     slices = ("v", (2, 3, 3, 4, 2, 4, 128))
-    c, r = call(steep_kernel, acc, [u], us=1.5)
+    u, c, r = call(steep_kernel, [("v", whole), *acc], [("v", u)], (), {0: 0}, us=1.3)
+    u = ("v", u)
     c, r, uz4 = call(top_kernel, [*acc, mat18], [u, ht, ("v", c), ("v", r)], (), {2: 0, 3: 1}, us=0.5)
     ft, ab, zt, nt, s = call(
         time_kernel,
@@ -565,8 +579,15 @@
     )
     s1, s3, s2 = in_row(s, 1), in_row(s, 3), in_row(s, 2)
     ft = ("v", from_ahead(ft, "tm", -1))
-    edges = ("v", (48, 32, 128))
-    c, r, x = call(flat_kernel, [*acc, edges], [u, low, high, ("v", ab), ("v", c), ("v", r), ("v", s)], (), {4: 0, 5: 1}, us=2.6)
+    edges = ("v", (32, 32, 128))
+    c, r, x = call(
+        flat_kernel,
+        [*acc, edges],
+        [u, low, high, ("v", ab), ("v", c), ("v", r), ("v", s)],
+        [VMEM((2, 2, 3, 3, 32, 128), F32)],
+        {4: 0, 5: 1},
+        us=2.2,
+    )
     head, tail, row = call(join_kernel, [mat18] * 3, [("v", s), ("v", s1), ("v", s2), ("v", s3)], us=0.1)
     row = from_ahead(row, "tm", ROW)
     stage = VMEM((3, 2, 3, 3, 4, 2, 4, 128), F32)

time: 34.2 us -> 34 us (level)
  Pallas kernels: 9.04 us -> 8.53 us
    pallas_call x8, Pallas kernels: 9.04 us -> 8.53 us  [call(): pl.pallas_call(kernel, out_shape=shapes, in_specs=[spec(k) for k, _ in ar...]
    ppermute x6, waiting for transfers between devices: 0.65 us -> 1.03 us  [from_ahead(): return lax.ppermute(x, axis, [(i, (i - k) % n) for i in range(n)])]
  transfers between devices with their start and end apart: 10 -> 10, of which waited for: 4 -> 4; matrix products, arithmetic and copies ran while one was open for 0% -> 0% of each run, Pallas kernels for 19% -> 18%
where the time goes in v4:
time: 34 us; the launch traced here: 33.3 us
  starting transfers between devices  14.3 us (42%)
  waiting for transfers between devices  9.75 us (29%)
  Pallas kernels  8.53 us (25%)
  between operations  0.72 us (2%)
    ppermute x6, starting transfers between devices, from_ahead(): return lax.ppermute(x, axis, [(i, (i - k) % n) for i in range(n)])  11 us
    pallas_call x8, Pallas kernels, call(): pl.pallas_call(kernel, out_shape=shapes, in_specs=[spec(k) for k, _ in ar...  8.53 us
    ppermute x1, waiting for transfers between devices, diagonal(): return lax.ppermute(x, ('space', 'tm'), pairs)  5.96 us
    ppermute x3, starting transfers between devices, in_row(): lax.ppermute(x, 'tm', [(i, i // ROW * ROW + (i - k) % ROW) for i in range...  3.3 us
    ppermute x3, waiting for transfers between devices, in_row(): lax.ppermute(x, 'tm', [(i, i // ROW * ROW + (i - k) % ROW) for i in range...  2.76 us
    ppermute x6, waiting for transfers between devices, from_ahead(): return lax.ppermute(x, axis, [(i, (i - k) % n) for i in range(n)])  1.03 us
  transfers between devices with their start and end apart: 10, of which 4 were waited for; matrix products, arithmetic and copies ran while one was open for 0% of the time, Pallas kernels for 18%

profile of v4, /device:TPU:0, one launch (start us, length us, event | category | flops | bytes accessed | tf_op | source)
XLA Modules:
  0.0 33.3 jit_solution(17393454239121481088)
XLA Ops:
  0.6 1.2 %shard_map.38 = (f32[4,2,3,3,4,2,4,128]{7,6,5,4,3,2,1,0:T(4,128)S(1)}, f32[36,8,128]{2,1,0:T(8,128)S(1)}, f32[12,8,128]{2,1,0:T(8,128)S(1)}, f32[24,8,128]{2,1,0...) custom-call(f32[4,2,3,3,4,2,4,128]{7,6,5,4,3,2,1,0:T(4,128)} %bitcast.12), custom_call_target="tpu_custom_call" | custom-call | flops 1000000 | bytes 3000000 | tf_op jit(solution)/shard_map/pallas_call | solution.py:515
  1.8 0.1 collective-permute-start.1
  1.9 4.0 %collective-permute-start.2 = (f32[36,8,128]{2,1,0:T(8,128)S(1)}, f32[36,8,128]{2,1,0:T(8,128)S(1)}, u32[]{:S(2)}, u32[]{:S(2)}) collective-permute-start(f32[36,8,128]{2,1,0:T(8,128)S(1)} %get-tuple-element.32), channel_id=1, source_target_pairs={{0,7},{1,0},{2,1},{3,2},{4,3},{5,4},{6,5},{7,6},{8,15},{9,8},{10,9... | collective-permute-start | bytes 442376 | tf_op jit(solution)/shard_map/ppermute | solution.py:529
  5.9 5.6 %collective-permute-start.3 = (f32[12,8,128]{2,1,0:T(8,128)S(1)}, f32[12,8,128]{2,1,0:T(8,128)S(1)}, u32[]{:S(2)}, u32[]{:S(2)}) collective-permute-start(f32[12,8,128]{2,1,0:T(8,128)S(1)} %get-tuple-element.36), channel_id=1, source_target_pairs={{0,120},{8,0},{16,8},{24,16},{32,24},{40,32},{48,40},{56,48},{64,5... | collective-permute-start | bytes 147464 | tf_op jit(solution)/shard_map/ppermute | solution.py:529
  11.5 0.0 collective-permute-start.4
  11.5 1.3 %shard_map.39 = (f32[4,2,3,3,4,2,4,128]{7,6,5,4,3,2,1,0:T(4,128)S(1)}, f32[4,8,4,8,128]{4,3,2,1,0:T(8,128)S(1)}, f32[4,8,5,8,128]{4,3,2,1,0:T(8,128)S(1)}) custom-call(f32[4,2,3,3,4,2,4,128]{7,6,5,4,3,2,1,0:T(4,128)S(1)} %get-tuple-element.28.u_in), custom_call_target="tpu_custom_call", output_to_operand_aliasing={{0}: (0, {})} | custom-call | flops 1300000 | bytes 3900000 | tf_op jit(solution)/shard_map/pallas_call | solution.py:515
  12.8 0.0 collective-permute-done.2.ht_ref
  12.8 0.4 %shard_map.40 = (f32[4,8,4,8,128]{4,3,2,1,0:T(8,128)S(1)}, f32[4,8,5,8,128]{4,3,2,1,0:T(8,128)S(1)}, f32[2,3,3,8,128]{4,3,2,1,0:T(8,128)S(1)}) custom-call(f32[4,2,3,3,4,2,4,128]{7,6,5,4,3,2,1,0:T(4,128)S(1)} %get-tuple-element.29.u_ref, f32[36,8,128]{2,1,0:T(8,128)S(1)} %collective-permute-done.2.ht_ref, ...), custom_call_target="tpu_custom_call", output_to_operand_aliasing={{0}: (2, {}), {1}: (3, {})} | custom-call | flops 500000 | bytes 1500000 | tf_op jit(solution)/shard_map/pallas_call | solution.py:515
  13.1 6.0 %collective-permute-done.4.corner_ref = f32[24,128]{1,0:T(8,128)S(1)} collective-permute-done((f32[24,128]{1,0:T(8,128)S(1)}, f32[24,128]{1,0:T(8,128)S(1)}, u32[]{:S(2)}, u32[]{:S(2)}) %collective-permute-start.4) | collective-permute-done | bytes 12320 | tf_op jit(solution)/shard_map/ppermute | solution.py:535
  19.1 0.0 collective-permute-done.3.lowt_ref
  19.1 0.0 collective-permute-done.1.high_ref
  19.1 0.7 %shard_map.41 = (f32[24,8,128]{2,1,0:T(8,128)S(1)}, f32[16,8,128]{2,1,0:T(8,128)S(1)}, f32[2,3,3,4,2,4,128]{6,5,4,3,2,1,0:T(4,128)S(1)}, f32[2,3,3,4,2,4,128]{6,...) custom-call(f32[4,2,3,3,4,2,4,128]{7,6,5,4,3,2,1,0:T(4,128)S(1)} %get-tuple-element.29.u_ref, ...), custom_call_target="tpu_custom_call" | custom-call | flops 700000 | bytes 2100000 | tf_op jit(solution)/shard_map/pallas_call | solution.py:515
  19.8 0.1 collective-permute-start.8
  19.9 2.4 %collective-permute-start.7 = (f32[2,3,3,8,128]{4,3,2,1,0:T(8,128)S(1)}, f32[2,3,3,8,128]{4,3,2,1,0:T(8,128)S(1)}, u32[]{:S(2)}, u32[]{:S(2)}) collective-permute-start(f32[2,3,3,8,128]{4,3,2,1,0:T(8,128)S(1)} %get-tuple-element.41.after_ref.s0_ref), channel_id=1, source_target_pairs={{0,2},{1,3},{2,0},{3,1},{4,6},{5,7},{6,4},{7,5},{8,10},{9,11},{10,... | collective-permute-start | bytes 221192 | tf_op jit(solution)/shard_map/ppermute | solution.py:540
  22.3 0.8 %collective-permute-start.6 = (f32[2,3,3,8,128]{4,3,2,1,0:T(8,128)S(1)}, f32[2,3,3,8,128]{4,3,2,1,0:T(8,128)S(1)}, u32[]{:S(2)}, u32[]{:S(2)}) collective-permute-start(f32[2,3,3,8,128]{4,3,2,1,0:T(8,128)S(1)} %get-tuple-element.41.after_ref.s0_ref), channel_id=1, source_target_pairs={{0,3},{1,0},{2,1},{3,2},{4,7},{5,4},{6,5},{7,6},{8,11},{9,8},{10,9... | collective-permute-start | bytes 221192 | tf_op jit(solution)/shard_map/ppermute | solution.py:540
  23.1 0.0 collective-permute-start
  23.1 1.2 %collective-permute-start.5 = (f32[24,8,128]{2,1,0:T(8,128)S(1)}, f32[24,8,128]{2,1,0:T(8,128)S(1)}, u32[]{:S(2)}, u32[]{:S(2)}) collective-permute-start(f32[24,8,128]{2,1,0:T(8,128)S(1)} %get-tuple-element.43), channel_id=1, source_target_pairs={{0,1},{1,2},{2,3},{3,4},{4,5},{5,6},{6,7},{7,0},{8,9},{9,10},{10,1... | collective-permute-start | bytes 294920 | tf_op jit(solution)/shard_map/ppermute | solution.py:529
  24.3 1.9 %collective-permute-done.8.s3_ref = f32[2,3,3,8,128]{4,3,2,1,0:T(8,128)S(1)} collective-permute-done((f32[2,3,3,8,128]{4,3,2,1,0:T(8,128)S(1)}, f32[2,3,3,8,128]{4,3,2,1,0:T(8,128)S(1)}, u32[]{:S(2)}, u32[]{:S(2)}) %collective-permute-start.8) | collective-permute-done | bytes 73760 | tf_op jit(solution)/shard_map/ppermute | solution.py:540
  26.3 0.0 collective-permute-done.7.s2_ref
  26.3 0.9 %collective-permute-done.6.s1_ref = f32[2,3,3,8,128]{4,3,2,1,0:T(8,128)S(1)} collective-permute-done((f32[2,3,3,8,128]{4,3,2,1,0:T(8,128)S(1)}, f32[2,3,3,8,128]{4,3,2,1,0:T(8,128)S(1)}, u32[]{:S(2)}, u32[]{:S(2)}) %collective-permute-start.6) | collective-permute-done | bytes 73760 | tf_op jit(solution)/shard_map/ppermute | solution.py:540
  27.1 0.1 shard_map.44
  27.2 0.1 collective-permute-start.9
  27.4 0.0 collective-permute-done.low_ref
  27.4 2.1 %shard_map.42 = (f32[4,8,4,8,128]{4,3,2,1,0:T(8,128)S(1)}, f32[4,8,5,8,128]{4,3,2,1,0:T(8,128)S(1)}, f32[32,32,128]{2,1,0:T(8,128)S(1)}) custom-call(f32[4,2,3,3,4,2,4,128]{7,6,5,4,3,2,1,0:T(4,128)S(1)} %get-tuple-element.29.u_ref, f32[24,8,128]{2,1,0:T(8,128)S(1)} %collective-permute-done.low_ref, ...), custom_call_target="tpu_custom_call", output_to_operand_aliasing={{0}: (4, {}), {1}: (5, {})} | custom-call | flops 2200000 | bytes 6600000 | tf_op jit(solution)/shard_map/pallas_call | solution.py:515
  29.4 1.0 %collective-permute-done.5.ft_ref = f32[24,8,128]{2,1,0:T(8,128)S(1)} collective-permute-done((f32[24,8,128]{2,1,0:T(8,128)S(1)}, f32[24,8,128]{2,1,0:T(8,128)S(1)}, u32[]{:S(2)}, u32[]{:S(2)}) %collective-permute-start.5) | collective-permute-done | bytes 98336 | tf_op jit(solution)/shard_map/ppermute | solution.py:529
  30.5 2.1 %shard_map.43 = (f32[4,2,3,3,4,2,4,128]{7,6,5,4,3,2,1,0:T(4,128)}, f32[4,2,3,3,4,2,4,128]{7,6,5,4,3,2,1,0:T(4,128)}) custom-call(f32[4,2,3,3,4,2,4,128]{7,6,5,4,3,2,1,0:T(4,128)S(1)} %get-tuple-element.29.u_ref, f32[32,32,128]{2,1,0:T(8,128)S(1)} %get-tuple-element.42.x_ref, f32[24,8,128]{2,1,0:T(8,128)S(1)} %collective-permute-done.5.ft_ref, ...), custom_call_target="tpu_custom_call" | custom-call | flops 3000000 | bytes 9000000 | tf_op jit(solution)/shard_map/pallas_call | solution.py:515
  32.6 0.0 collective-permute-done.9.row_ref
  32.6 0.7 %shard_map.45 = f32[2,3,3,2,4,128]{5,4,3,2,1,0:T(4,128)} custom-call(f32[2,3,3,8,128]{4,3,2,1,0:T(8,128)S(1)} %get-tuple-element.50.head_ref, f32[2,3,3,8,128]{4,3,2,1,0:T(8,128)S(1)} %collective-permute-done.9.row_ref, f32[2,3,3,8,128]{4,3,2,1,0:T(8,128)S(1)} %get-tuple-element.52.tail_ref), custom_call_target="tpu_custom_call" | custom-call | flops 1000000 | bytes 3000000 | tf_op jit(solution)/shard_map/pallas_call | solution.py:515
Async XLA Ops:
  1.8 17.3 %collective-permute-start.1 = (f32[48,8,128]{2,1,0:T(8,128)S(1)}, f32[48,8,128]{2,1,0:T(8,128)S(1)}, u32[]{:S(2)}, u32[]{:S(2)}) collective-permute-start(f32[48,8,128]{2,1,0:T(8,128)S(1)} %get-tuple-element.31), channel_id=1, source_target_pairs={{0,8},{8,16},{16,24},{24,32},{32,40},{40,48},{48,56},{56,64},{64,7... | collective-permute-start | bytes 589832 | tf_op jit(solution)/shard_map/ppermute | solution.py:529
  1.9 10.8 %collective-permute-start.2 = (f32[36,8,128]{2,1,0:T(8,128)S(1)}, f32[36,8,128]{2,1,0:T(8,128)S(1)}, u32[]{:S(2)}, u32[]{:S(2)}) collective-permute-start(f32[36,8,128]{2,1,0:T(8,128)S(1)} %get-tuple-element.32), channel_id=1, source_target_pairs={{0,7},{1,0},{2,1},{3,2},{4,3},{5,4},{6,5},{7,6},{8,15},{9,8},{10,9... | collective-permute-start | bytes 442376 | tf_op jit(solution)/shard_map/ppermute | solution.py:529
  5.9 13.2 %collective-permute-start.3 = (f32[12,8,128]{2,1,0:T(8,128)S(1)}, f32[12,8,128]{2,1,0:T(8,128)S(1)}, u32[]{:S(2)}, u32[]{:S(2)}) collective-permute-start(f32[12,8,128]{2,1,0:T(8,128)S(1)} %get-tuple-element.36), channel_id=1, source_target_pairs={{0,120},{8,0},{16,8},{24,16},{32,24},{40,32},{48,40},{56,48},{64,5... | collective-permute-start | bytes 147464 | tf_op jit(solution)/shard_map/ppermute | solution.py:529
  11.5 7.6 %collective-permute-start.4 = (f32[24,128]{1,0:T(8,128)S(1)}, f32[24,128]{1,0:T(8,128)S(1)}, u32[]{:S(2)}, u32[]{:S(2)}) collective-permute-start(f32[24,128]{1,0:T(8,128)S(1)} %get-tuple-element.37), channel_id=1, source_target_pairs={{0,15},{1,8},{2,9},{3,10},{4,11},{5,12},{6,13},{7,14},{8,23},{9,16... | collective-permute-start | bytes 36872 | tf_op jit(solution)/shard_map/ppermute | solution.py:535
  19.8 6.4 %collective-permute-start.8 = (f32[2,3,3,8,128]{4,3,2,1,0:T(8,128)S(1)}, f32[2,3,3,8,128]{4,3,2,1,0:T(8,128)S(1)}, u32[]{:S(2)}, u32[]{:S(2)}) collective-permute-start(f32[2,3,3,8,128]{4,3,2,1,0:T(8,128)S(1)} %get-tuple-element.41.after_ref.s0_ref), channel_id=1, source_target_pairs={{0,1},{1,2},{2,3},{3,0},{4,5},{5,6},{6,7},{7,4},{8,9},{9,10},{10,1... | collective-permute-start | bytes 221192 | tf_op jit(solution)/shard_map/ppermute | solution.py:540
  19.9 6.3 %collective-permute-start.7 = (f32[2,3,3,8,128]{4,3,2,1,0:T(8,128)S(1)}, f32[2,3,3,8,128]{4,3,2,1,0:T(8,128)S(1)}, u32[]{:S(2)}, u32[]{:S(2)}) collective-permute-start(f32[2,3,3,8,128]{4,3,2,1,0:T(8,128)S(1)} %get-tuple-element.41.after_ref.s0_ref), channel_id=1, source_target_pairs={{0,2},{1,3},{2,0},{3,1},{4,6},{5,7},{6,4},{7,5},{8,10},{9,11},{10,... | collective-permute-start | bytes 221192 | tf_op jit(solution)/shard_map/ppermute | solution.py:540
  22.3 4.8 %collective-permute-start.6 = (f32[2,3,3,8,128]{4,3,2,1,0:T(8,128)S(1)}, f32[2,3,3,8,128]{4,3,2,1,0:T(8,128)S(1)}, u32[]{:S(2)}, u32[]{:S(2)}) collective-permute-start(f32[2,3,3,8,128]{4,3,2,1,0:T(8,128)S(1)} %get-tuple-element.41.after_ref.s0_ref), channel_id=1, source_target_pairs={{0,3},{1,0},{2,1},{3,2},{4,7},{5,4},{6,5},{7,6},{8,11},{9,8},{10,9... | collective-permute-start | bytes 221192 | tf_op jit(solution)/shard_map/ppermute | solution.py:540
  23.1 4.2 %collective-permute-start = (f32[24,8,128]{2,1,0:T(8,128)S(1)}, f32[24,8,128]{2,1,0:T(8,128)S(1)}, u32[]{:S(2)}, u32[]{:S(2)}) collective-permute-start(f32[24,8,128]{2,1,0:T(8,128)S(1)} %get-tuple-element.30), channel_id=1, source_target_pairs={{0,120},{8,0},{16,8},{24,16},{32,24},{40,32},{48,40},{56,48},{64,5... | collective-permute-start | bytes 294920 | tf_op jit(solution)/shard_map/ppermute | solution.py:529
  23.1 7.3 %collective-permute-start.5 = (f32[24,8,128]{2,1,0:T(8,128)S(1)}, f32[24,8,128]{2,1,0:T(8,128)S(1)}, u32[]{:S(2)}, u32[]{:S(2)}) collective-permute-start(f32[24,8,128]{2,1,0:T(8,128)S(1)} %get-tuple-element.43), channel_id=1, source_target_pairs={{0,1},{1,2},{2,3},{3,4},{4,5},{5,6},{6,7},{7,0},{8,9},{9,10},{10,1... | collective-permute-start | bytes 294920 | tf_op jit(solution)/shard_map/ppermute | solution.py:529
  27.2 5.4 %collective-permute-start.9 = (f32[2,3,3,8,128]{4,3,2,1,0:T(8,128)S(1)}, f32[2,3,3,8,128]{4,3,2,1,0:T(8,128)S(1)}, u32[]{:S(2)}, u32[]{:S(2)}) collective-permute-start(f32[2,3,3,8,128]{4,3,2,1,0:T(8,128)S(1)} %get-tuple-element.51), channel_id=1, source_target_pairs={{0,4},{1,5},{2,6},{3,7},{4,0},{5,1},{6,2},{7,3},{8,12},{9,13},{10,... | collective-permute-start | bytes 221192 | tf_op jit(solution)/shard_map/ppermute | solution.py:529
